TPU v7x, 128 devices: a whole 4x4x4 slice. The times are simulated.
128 devices in a mesh: replica: 4 (over x_lo, core), expert: 32 (over x_hi, z, y).
Axes of the slice: x: 4 (x_hi: 2, x_lo: 2; x = x_hi * 2 + x_lo), y: 4, z: 4, core: 2. Of those that a mesh axis runs over, the one named last changes fastest.
Arguments:
- tokens: bfloat16 [16384, 2048], P(('replica', 'expert')), may hold values from -6 to 6
- routing: int32 [16384, 8], P(('replica', 'expert')), may hold values from 0 to 31, all different within a row; in each aligned block of 128 rows (0 to 127, 128 to 255, ...) at most 40 rows name the same one
- gate_scores: float32 [16384, 8], P(('replica', 'expert')), may hold values from 0.1 to 1
- cotangent: bfloat16 [16384, 2048], P(('replica', 'expert')), may hold values from -48 to 48
- w_gate: bfloat16 [4, 32, 2048, 384], P('replica', 'expert'), may hold values from -6 to 6
- w_up: bfloat16 [4, 32, 2048, 384], P('replica', 'expert'), may hold values from -6 to 6
- w_down: bfloat16 [4, 32, 384, 2048], P('replica', 'expert'), may hold values from -6 to 6
- mom_gate: bfloat16 [4, 32, 2048, 384], P('replica', 'expert'), may hold values from -3 to 3
- mom_up: bfloat16 [4, 32, 2048, 384], P('replica', 'expert'), may hold values from -3 to 3
- mom_down: bfloat16 [4, 32, 384, 2048], P('replica', 'expert'), may hold values from -3 to 3
- gossip_round: int32 [32], P('expert'), may hold values from 0 to 1
Outputs:
- layer_out: bfloat16 [16384, 2048], P(('replica', 'expert'))
- token_grad: bfloat16 [16384, 2048], P(('replica', 'expert'))
- new_gate: bfloat16 [4, 32, 2048, 384], P('replica', 'expert')
- new_up: bfloat16 [4, 32, 2048, 384], P('replica', 'expert')
- new_down: bfloat16 [4, 32, 384, 2048], P('replica', 'expert')
- new_mom_gate: bfloat16 [4, 32, 2048, 384], P('replica', 'expert')
- new_mom_up: bfloat16 [4, 32, 2048, 384], P('replica', 'expert')
- new_mom_down: bfloat16 [4, 32, 384, 2048], P('replica', 'expert')
Inputs may be any that keep to these rules, and one draw needn't show every extreme that they name: `routing`: each token names 8 different experts; among the 128 tokens of one source no expert is named more than 40 times, a bound that some block reaches. `gossip_round`: each expert's round value names the bit distance of that expert's partner in this round.
All inputs are finite; a program needn't handle non-finite values.
Results may differ from a plain program's by a relative error of at most 0.0064.
Values may be sent and summed in bfloat16 or wider, within the bound.
A program may use at most 192 MiB of HBM per device.

v0:
```python
import jax
import jax.numpy as jnp
from jax import lax
from jax.sharding import PartitionSpec as P

momentum_beta = 0.9
learn_rate = 0.1


def partner_2(value, axis, stride):
    mask = 2**stride
    pairs = [(source, source ^ mask) for source in range(lax.axis_size(axis))]
    return lax.ppermute(value, axis, pairs)


def expert_forward(rows_in, weight_gate, weight_up, weight_down):
    scale_in = rows_in.shape[1] ** (-0.5)
    scale_hidden = weight_gate.shape[1] ** (-0.5)
    gate_pre = jnp.dot(rows_in, weight_gate, preferred_element_type=jnp.float32) * scale_in
    up_pre = jnp.dot(rows_in, weight_up, preferred_element_type=jnp.float32) * scale_in
    sigmoid_gate = jax.nn.sigmoid(gate_pre)
    activation = (gate_pre * sigmoid_gate * up_pre).astype(jnp.bfloat16)
    produced = (
        jnp.dot(activation, weight_down, preferred_element_type=jnp.float32) * scale_hidden
    ).astype(jnp.bfloat16)
    return (gate_pre, up_pre, sigmoid_gate, activation, produced)


def expert_backward(
    rows_in,
    rows_grad,
    weight_gate,
    weight_up,
    weight_down,
    gate_pre,
    up_pre,
    sigmoid_gate,
    activation,
):
    scale_in = rows_in.shape[1] ** (-0.5)
    scale_hidden = weight_gate.shape[1] ** (-0.5)
    inner_dims = (((1,), (1,)), ((), ()))
    outer_dims = (((0,), (0,)), ((), ()))
    grad_act = (
        lax.dot_general(rows_grad, weight_down, inner_dims, preferred_element_type=jnp.float32)
        * scale_hidden
    )
    grad_gate_pre = (
        grad_act * up_pre * sigmoid_gate * (1.0 + gate_pre * (1.0 - sigmoid_gate))
    ).astype(jnp.bfloat16)
    grad_up_pre = (grad_act * gate_pre * sigmoid_gate).astype(jnp.bfloat16)
    grad_down = (
        lax.dot_general(activation, rows_grad, outer_dims, preferred_element_type=jnp.float32)
        * scale_hidden
    )
    grad_gate = (
        lax.dot_general(rows_in, grad_gate_pre, outer_dims, preferred_element_type=jnp.float32)
        * scale_in
    )
    grad_up = (
        lax.dot_general(rows_in, grad_up_pre, outer_dims, preferred_element_type=jnp.float32)
        * scale_in
    )
    back_sum = lax.dot_general(
        grad_gate_pre, weight_gate, inner_dims, preferred_element_type=jnp.float32
    )
    back_sum = back_sum + lax.dot_general(
        grad_up_pre, weight_up, inner_dims, preferred_element_type=jnp.float32
    )
    rows_back = (back_sum * scale_in).astype(jnp.bfloat16)
    return (rows_back, grad_gate, grad_up, grad_down)


def momentum_step(weight, moment, gradient):
    moment_new = momentum_beta * moment.astype(jnp.float32) + gradient
    weight_new = (weight.astype(jnp.float32) - learn_rate * moment_new).astype(jnp.bfloat16)
    return (weight_new, moment_new.astype(jnp.bfloat16))


def per_device(
    tokens,
    routing,
    gate_scores,
    cotangent,
    w_gate,
    w_up,
    w_down,
    mom_gate,
    mom_up,
    mom_down,
    gossip_round,
):
    tok_rows, feature_width = tokens.shape
    top_count = routing.shape[1]
    experts = lax.axis_size("expert")
    capacity = max(2, min(tok_rows, tok_rows * top_count // experts + 8))
    gate_share = gate_scores / jnp.sum(gate_scores, axis=1, keepdims=True)
    expert_ids = routing.reshape(-1)
    member = (expert_ids[:, None] == jnp.arange(experts, dtype=jnp.int32)[None, :]).astype(
        jnp.int32
    )
    earlier = jnp.sum((jnp.cumsum(member, axis=0) - member) * member, axis=1)
    target = expert_ids * capacity + earlier
    source = jnp.arange(expert_ids.shape[0], dtype=jnp.int32) // top_count
    send_rows = (
        jnp.zeros((experts * capacity, feature_width), jnp.bfloat16).at[target].set(tokens[source])
    )
    weighted = (gate_share.reshape(-1)[:, None] * cotangent[source].astype(jnp.float32)).astype(
        jnp.bfloat16
    )
    send_grad = (
        jnp.zeros((experts * capacity, feature_width), jnp.bfloat16).at[target].set(weighted)
    )
    arrived = lax.all_to_all(
        send_rows.reshape(experts, capacity, feature_width),
        "expert",
        split_axis=0,
        concat_axis=0,
        tiled=True,
    ).reshape(-1, feature_width)
    arrived_grad = lax.all_to_all(
        send_grad.reshape(experts, capacity, feature_width),
        "expert",
        split_axis=0,
        concat_axis=0,
        tiled=True,
    ).reshape(-1, feature_width)
    weight_gate = w_gate[0, 0]
    weight_up = w_up[0, 0]
    weight_down = w_down[0, 0]
    gate_pre, up_pre, sigmoid_gate, activation, produced = expert_forward(
        arrived, weight_gate, weight_up, weight_down
    )
    returned = lax.all_to_all(
        produced.reshape(experts, capacity, feature_width),
        "expert",
        split_axis=0,
        concat_axis=0,
        tiled=True,
    ).reshape(-1, feature_width)
    picked = returned[target].astype(jnp.float32) * gate_share.reshape(-1)[:, None]
    layer_out = jnp.sum(picked.reshape(tok_rows, top_count, feature_width), axis=1).astype(
        jnp.bfloat16
    )
    rows_back, grad_gate, grad_up, grad_down = expert_backward(
        arrived,
        arrived_grad,
        weight_gate,
        weight_up,
        weight_down,
        gate_pre,
        up_pre,
        sigmoid_gate,
        activation,
    )
    returned_grad = lax.all_to_all(
        rows_back.reshape(experts, capacity, feature_width),
        "expert",
        split_axis=0,
        concat_axis=0,
        tiled=True,
    ).reshape(-1, feature_width)
    picked_back = returned_grad[target].astype(jnp.float32)
    token_grad = jnp.sum(picked_back.reshape(tok_rows, top_count, feature_width), axis=1).astype(
        jnp.bfloat16
    )
    gate_new, gate_moment = momentum_step(weight_gate, mom_gate[0, 0], grad_gate)
    up_new, up_moment = momentum_step(weight_up, mom_up[0, 0], grad_up)
    down_new, down_moment = momentum_step(weight_down, mom_down[0, 0], grad_down)
    hidden_width = weight_gate.shape[1]
    stacked = jnp.stack([gate_new, up_new, down_new.reshape(feature_width, hidden_width)], axis=0)
    bit_count = lax.axis_size("replica").bit_length() - 1
    bit_now = gossip_round[0] % bit_count
    partner = stacked
    for bit_index in range(bit_count):
        swapped = partner_2(stacked, "replica", bit_index)
        partner = jnp.where(bit_now == bit_index, swapped, partner)
    averaged = ((stacked.astype(jnp.float32) + partner.astype(jnp.float32)) * 0.5).astype(
        jnp.bfloat16
    )
    new_gate = averaged[0][None, None]
    new_up = averaged[1][None, None]
    new_down = averaged[2].reshape(hidden_width, feature_width)[None, None]
    return (
        layer_out,
        token_grad,
        new_gate,
        new_up,
        new_down,
        gate_moment[None, None],
        up_moment[None, None],
        down_moment[None, None],
    )


def solution(mesh):
    placed = (
        P(("replica", "expert"), None),
        P(("replica", "expert"), None),
        P(("replica", "expert"), None),
        P(("replica", "expert"), None),
        P("replica", "expert", None, None),
        P("replica", "expert", None, None),
        P("replica", "expert", None, None),
        P("replica", "expert", None, None),
        P("replica", "expert", None, None),
        P("replica", "expert", None, None),
        P("expert"),
    )
    return jax.shard_map(
        per_device,
        mesh=mesh,
        in_specs=placed,
        out_specs=(
            P(("replica", "expert"), None),
            P(("replica", "expert"), None),
            P("replica", "expert", None, None),
            P("replica", "expert", None, None),
            P("replica", "expert", None, None),
            P("replica", "expert", None, None),
            P("replica", "expert", None, None),
            P("replica", "expert", None, None),
        ),
        check_vma=False,
    )
```

profile of v0, /device:TPU:50, one launch (start us, length us, event | category | flops | bytes accessed | tf_op | source)
XLA Modules:
  0.0 469.0 jit_solution(11122694127658707902)
XLA Ops:
  0.7 0.7 broadcast_multiply_fusion
  1.4 0.8 copy.21
  2.6 9.0 %reduce-window.6 = s32[32,8,128]{2,1,0:T(8,128)S(1)} reduce-window(s32[32,8,128]{2,1,0:T(8,128)S(1)} %fusion.19, s32[]{:T(128)} %constant.24.clone.1), window={size=1x1x128 pad=0_0x0_0x127_0}, to_apply=%region_0.0 | reduce-window | flops 4161536 | bytes 262148 | tf_op jit(solution)/shard_map/reduce-window
  12.2 23.6 %scatter_custom_fusion = bf16[1280,2048]{1,0:T(8,128)(2,1)} fusion(s32[1024]{0:T(1024)S(1)} %bitcast.103, bf16[128,2048]{1,0:T(8,128)(2,1)S(1)} %copy-done, s32[1024]{0:T(1024)S(1)} %broadcast_clamp_fusion.1, bf16[]{:T(256)} %constant.21.clone.1), kind=kCustom, calls=%fused_computation.15 | custom fusion | bytes 5242882 | tf_op jit(solution)/shard_map/scatter | solution.py:106
  35.8 9.7 %all-to-all-start = ((bf16[32,40,2048]{2,1,0:T(8,128)(2,1)}), bf16[32,40,2048]{2,1,0:T(8,128)(2,1)}, u32[]{:S(2)}, u32[]{:S(2)}) async-start(bf16[32,40,2048]{2,1,0:T(8,128)(2,1)} %bitcast.96), calls=%async_computation | async-start | bytes 10485760 | tf_op jit(solution)/shard_map/all_to_all | solution.py:114
  45.8 23.5 %scatter_custom_fusion.1 = bf16[1280,2048]{1,0:T(8,128)(2,1)} fusion(s32[1024]{0:T(1024)S(1)} %bitcast.104, f32[1024]{0:T(1024)S(1)} %mul.149, bf16[]{:T(256)} %constant.21.clone.1, bf16[128,2048]{1,0:T(8,128)(2,1)S(1)} %copy-done.11, s32[1024]{0:T(1024)S(1)} %broadcast_clamp_fusion.1), kind=kCustom, calls=%fused_computation.13 | custom fusion | flops 6291456 | bytes 5775362 | tf_op jit(solution)/shard_map/scatter | solution.py:112
  69.3 47.4 %all-to-all-done = bf16[32,40,2048]{2,1,0:T(8,128)(2,1)} async-done(((bf16[32,40,2048]{2,1,0:T(8,128)(2,1)}), bf16[32,40,2048]{2,1,0:T(8,128)(2,1)}, u32[]{:S(2)}, u32[]{:S(2)}) %all-to-all-start) | async-done | bytes 5242912 | tf_op jit(solution)/shard_map/all_to_all | solution.py:114
  116.8 9.3 %all-to-all-start.2 = ((bf16[32,40,2048]{2,1,0:T(8,128)(2,1)}), bf16[32,40,2048]{2,1,0:T(8,128)(2,1)}, u32[]{:S(2)}, u32[]{:S(2)}) async-start(bf16[32,40,2048]{2,1,0:T(8,128)(2,1)} %bitcast.97), calls=%async_computation.2 | async-start | bytes 10485760 | tf_op jit(solution)/shard_map/all_to_all | solution.py:121
  126.0 6.8 %convolution_multiply_fusion.1 = f32[1280,384]{1,0:T(8,128)} fusion(bf16[1280,2048]{1,0:T(8,128)(2,1)} %bitcast.6, bf16[1,1,2048,384]{3,2,1,0:T(8,128)(2,1)S(1)} %copy-done.7), kind=kOutput, calls=%fused_computation.25 | convolution fusion | flops 2013757440 | bytes 8781824 | tf_op jit(solution)/shard_map/dot_general | solution.py:20
  132.8 6.8 %convolution_multiply_fusion.2 = f32[1280,384]{1,0:T(8,128)} fusion(bf16[1280,2048]{1,0:T(8,128)(2,1)} %bitcast.6, bf16[1,1,2048,384]{3,2,1,0:T(8,128)(2,1)S(1)} %copy-done.5), kind=kOutput, calls=%fused_computation.26 | convolution fusion | flops 2013757440 | bytes 8781824 | tf_op jit(solution)/shard_map/dot_general | solution.py:19
  139.6 57.6 %all-to-all-done.2 = bf16[32,40,2048]{2,1,0:T(8,128)(2,1)} async-done(((bf16[32,40,2048]{2,1,0:T(8,128)(2,1)}), bf16[32,40,2048]{2,1,0:T(8,128)(2,1)}, u32[]{:S(2)}, u32[]{:S(2)}) %all-to-all-start.2) | async-done | bytes 5242912 | tf_op jit(solution)/shard_map/all_to_all | solution.py:121
  197.2 8.6 %multiply_convert_fusion.5 = (bf16[1280,384]{1,0:T(8,128)(2,1)}, bf16[1280,384]{1,0:T(8,128)(2,1)}, bf16[1280,384]{1,0:T(8,128)(2,1)S(1)}) fusion(f32[1280,384]{1,0:T(8,128)} %convolution_multiply_fusion.2, f32[1280,384]{1,0:T(8,128)} %convolution_multiply_fusion.1, bf16[1280,2048]{1,0:T(8,128)(2,1)} %bitcast.14, bf16[1,1,384,2048]{3,2,1,0:T(8,128)(2,1)S(1)} %copy-done.4), kind=kOutput, calls=%fused_computation.29 | convolution fusion | flops 2021621760 | bytes 13697024 | tf_op jit(solution)/shard_map/dot_general | solution.py:45
  205.9 4.6 multiply_convert_fusion.1
  210.5 9.6 %all-to-all-start.1 = ((bf16[32,40,2048]{2,1,0:T(8,128)(2,1)}), bf16[32,40,2048]{2,1,0:T(8,128)(2,1)}, u32[]{:S(2)}, u32[]{:S(2)}) async-start(bf16[32,40,2048]{2,1,0:T(8,128)(2,1)} %bitcast.99), calls=%async_computation.1 | async-start | bytes 10485760 | tf_op jit(solution)/shard_map/all_to_all | solution.py:134
  220.1 7.5 %convert_bitcast_fusion = (bf16[1,1,384,2048]{3,2,1,0:T(8,128)(2,1)}, bf16[384,2048]{1,0:T(8,128)(2,1)}) fusion(bf16[1,1,384,2048]{3,2,1,0:T(8,128)(2,1)S(1)} %copy-done.4, bf16[1280,384]{1,0:T(8,128)(2,1)S(1)} %get-tuple-element.13, bf16[1280,2048]{1,0:T(8,128)(2,1)} %bitcast.14, bf16[1,1,384,2048]{3,2,1,0:T(8,128)(2,1)} %param.20), kind=kOutput, calls=%fused_computation.44 | convolution fusion | flops 2020343808 | bytes 12517376 | tf_op jit(solution)/shard_map/dot_general | solution.py:53
  227.6 3.3 stack_reshape.3
  230.9 6.2 %bitcast_add_fusion.1 = f32[2048,384]{1,0:T(8,128)S(1)} fusion(bf16[1,1,2048,384]{3,2,1,0:T(8,128)(2,1)} %param.19, bf16[1280,2048]{1,0:T(8,128)(2,1)} %bitcast.6, bf16[1280,384]{1,0:T(8,128)(2,1)S(1)} %copy-done.10), kind=kOutput, calls=%fused_computation.19 | convolution fusion | flops 2016411648 | bytes 10944512 | tf_op jit(solution)/shard_map/dot_general | solution.py:61
  237.2 8.4 %convert_bitcast_fusion.1 = (bf16[1,1,2048,384]{3,2,1,0:T(8,128)(2,1)}, bf16[1,2048,384]{2,1,0:T(8,128)(2,1)S(1)}, bf16[1,2048,384]{2,1,0:T(8,128)(2,1)S(1)}, bf16[1,1,2048,384]{3,2,1,0:T(8,128)(2,1)}) fusion(f32[2048,384]{1,0:T(8,128)S(1)} %bitcast_add_fusion.1, bf16[1,1,2048,384]{3,2,1,0:T(8,128)(2,1)S(1)} %copy-done.8, ...), kind=kOutput, calls=%fused_computation.45 | convolution fusion | flops 2024275968 | bytes 20381696 | tf_op jit(solution)/shard_map/dot_general | solution.py:57
  245.5 2.7 pad_maximum_fusion
  249.1 2.9 fusion.13
  252.0 4.8 %multiply_convert_fusion = bf16[1280,2048]{1,0:T(8,128)(2,1)} fusion(f32[1280,2048]{1,0:T(8,128)S(1)} %fusion.13, bf16[1280,384]{1,0:T(8,128)(2,1)S(1)} %copy-done.10, bf16[1,1,2048,384]{3,2,1,0:T(8,128)(2,1)S(1)} %copy-done.8), kind=kOutput, calls=%fused_computation.6 | convolution fusion | flops 2021130240 | bytes 18284544 | tf_op jit(solution)/shard_map/dot_general | solution.py:67
  256.8 35.7 %all-to-all-done.1 = bf16[32,40,2048]{2,1,0:T(8,128)(2,1)} async-done(((bf16[32,40,2048]{2,1,0:T(8,128)(2,1)}), bf16[32,40,2048]{2,1,0:T(8,128)(2,1)}, u32[]{:S(2)}, u32[]{:S(2)}) %all-to-all-start.1) | async-done | bytes 5242912 | tf_op jit(solution)/shard_map/all_to_all | solution.py:134
  292.5 7.8 %all-to-all-start.3 = ((bf16[32,40,2048]{2,1,0:T(8,128)(2,1)}), bf16[32,40,2048]{2,1,0:T(8,128)(2,1)}, u32[]{:S(2)}, u32[]{:S(2)}) async-start(bf16[32,40,2048]{2,1,0:T(8,128)(2,1)} %bitcast.98), calls=%async_computation.3 | async-start | bytes 10485760 | tf_op jit(solution)/shard_map/all_to_all | solution.py:156
  300.9 81.6 %collective-permute-done = bf16[3,2048,384]{2,1,0:T(8,128)(2,1)} collective-permute-done((bf16[3,2048,384]{2,1,0:T(8,128)(2,1)}, bf16[3,2048,384]{2,1,0:T(8,128)(2,1)}, u32[]{:S(2)}, u32[]{:S(2)}) %collective-permute-start) | collective-permute-done | bytes 4718624 | tf_op jit(solution)/shard_map/ppermute | solution.py:13
  382.5 5.1 %multiply_convert_fusion.2 = bf16[3,2048,384]{2,1,0:T(8,128)(2,1)S(1)} fusion(bf16[3,2048,384]{2,1,0:T(8,128)(2,1)} %collective-permute-done, bf16[3,2048,384]{2,1,0:T(8,128)(2,1)} %collective-permute-done.1, pred[]{:T(512)S(6)} %eq.42, pred[]{:T(512)S(6)} %eq.41, bf16[1,2048,384]{2,1,0:T(8,128)(2,1)S(1)} %stack_reshape.3, ...), kind=kLoop, calls=%fused_computation.8 | loop fusion | flops 21233664 | bytes 18874370 | tf_op jit(solution)/shard_map/convert_element_type | solution.py:178
  387.6 2.1 fusion.21
  389.7 2.6 broadcast_in_dim_reshape_squeeze.3
  392.4 12.0 %gather_fusion = bf16[1024,2048]{1,0:T(8,128)(2,1)} fusion(bf16[1280,2048]{1,0:T(8,128)(2,1)} %bitcast.11, s32[1024]{0:T(1024)S(1)} %broadcast_clamp_fusion), kind=kCustom, calls=%fused_computation.1 | custom fusion | bytes 8392704 | tf_op jit(solution)/shard_map/gather | solution.py:141
  404.4 7.3 %fusion = bf16[128,2048]{1,0:T(8,128)(2,1)} fusion(bf16[1024,2048]{1,0:T(8,128)(2,1)} %gather_fusion, f32[128,8]{1,0:T(8,128)S(1)} %copy.25), kind=kLoop, calls=%fused_computation.10 | loop fusion | flops 6029312 | bytes 4722688 | tf_op jit(solution)/shard_map/reduce_sum | solution.py:142
  411.7 39.1 %all-to-all-done.3 = bf16[32,40,2048]{2,1,0:T(8,128)(2,1)} async-done(((bf16[32,40,2048]{2,1,0:T(8,128)(2,1)}), bf16[32,40,2048]{2,1,0:T(8,128)(2,1)}, u32[]{:S(2)}, u32[]{:S(2)}) %all-to-all-start.3) | async-done | bytes 5242912 | tf_op jit(solution)/shard_map/all_to_all | solution.py:156
  450.8 12.2 %gather_fusion.1 = bf16[1024,2048]{1,0:T(8,128)(2,1)} fusion(bf16[1280,2048]{1,0:T(8,128)(2,1)} %bitcast.16, s32[1024]{0:T(1024)S(1)} %broadcast_clamp_fusion), kind=kCustom, calls=%fused_computation.3 | custom fusion | bytes 8392704 | tf_op jit(solution)/shard_map/gather | solution.py:163
  463.0 5.9 %bitcast_reduce_fusion = bf16[128,2048]{1,0:T(8,128)(2,1)} fusion(bf16[1024,2048]{1,0:T(8,128)(2,1)} %gather_fusion.1), kind=kLoop, calls=%fused_computation.14 | loop fusion | flops 1835008 | bytes 4718592 | tf_op jit(solution)/shard_map/reduce_sum | solution.py:164
  (51 shorter events, 2.0 us)
Async XLA Ops:
  0.6 11.5 %copy-start = (bf16[128,2048]{1,0:T(8,128)(2,1)S(1)}, bf16[128,2048]{1,0:T(8,128)(2,1)}, u32[]{:S(2)}) copy-start(bf16[128,2048]{1,0:T(8,128)(2,1)} %param.11) | copy-start | bytes 1572868
  35.8 9.8 %copy-start.12 = (f32[128,8]{0,1:T(8,128)S(1)}, f32[128,8]{0,1:T(8,128)}, u32[]{:S(2)}) copy-start(f32[128,8]{0,1:T(8,128)} %param.13) | copy-start | bytes 12292
  35.8 10.0 %copy-start.11 = (bf16[128,2048]{1,0:T(8,128)(2,1)S(1)}, bf16[128,2048]{1,0:T(8,128)(2,1)}, u32[]{:S(2)}) copy-start(bf16[128,2048]{1,0:T(8,128)(2,1)} %param.14) | copy-start | bytes 1572868
  35.8 81.0 %all-to-all-start = ((bf16[32,40,2048]{2,1,0:T(8,128)(2,1)}), bf16[32,40,2048]{2,1,0:T(8,128)(2,1)}, u32[]{:S(2)}, u32[]{:S(2)}) async-start(bf16[32,40,2048]{2,1,0:T(8,128)(2,1)} %bitcast.96), calls=%async_computation | async-start | bytes 10485760 | tf_op jit(solution)/shard_map/all_to_all | solution.py:114
  116.8 9.3 %copy-start.7 = (bf16[1,1,2048,384]{3,2,1,0:T(8,128)(2,1)S(1)}, bf16[1,1,2048,384]{3,2,1,0:T(8,128)(2,1)}, u32[]{:S(2)}) copy-start(bf16[1,1,2048,384]{3,2,1,0:T(8,128)(2,1)} %param.16) | copy-start | bytes 4718596
  116.8 80.5 %all-to-all-start.2 = ((bf16[32,40,2048]{2,1,0:T(8,128)(2,1)}), bf16[32,40,2048]{2,1,0:T(8,128)(2,1)}, u32[]{:S(2)}, u32[]{:S(2)}) async-start(bf16[32,40,2048]{2,1,0:T(8,128)(2,1)} %bitcast.97), calls=%async_computation.2 | async-start | bytes 10485760 | tf_op jit(solution)/shard_map/all_to_all | solution.py:121
  126.0 6.8 %copy-start.5 = (bf16[1,1,2048,384]{3,2,1,0:T(8,128)(2,1)S(1)}, bf16[1,1,2048,384]{3,2,1,0:T(8,128)(2,1)}, u32[]{:S(2)}) copy-start(bf16[1,1,2048,384]{3,2,1,0:T(8,128)(2,1)} %param.15) | copy-start | bytes 4718596
  132.8 64.4 %copy-start.4 = (bf16[1,1,384,2048]{3,2,1,0:T(8,128)(2,1)S(1)}, bf16[1,1,384,2048]{3,2,1,0:T(8,128)(2,1)}, u32[]{:S(2)}) copy-start(bf16[1,1,384,2048]{3,2,1,0:T(8,128)(2,1)} %param.17) | copy-start | bytes 4718596
  210.5 82.0 %all-to-all-start.1 = ((bf16[32,40,2048]{2,1,0:T(8,128)(2,1)}), bf16[32,40,2048]{2,1,0:T(8,128)(2,1)}, u32[]{:S(2)}, u32[]{:S(2)}) async-start(bf16[32,40,2048]{2,1,0:T(8,128)(2,1)} %bitcast.99), calls=%async_computation.1 | async-start | bytes 10485760 | tf_op jit(solution)/shard_map/all_to_all | solution.py:134
  227.6 3.3 copy-start.10
  230.9 6.2 %copy-start.6 = (bf16[1,1,2048,384]{3,2,1,0:T(8,128)(2,1)S(1)}, bf16[1,1,2048,384]{3,2,1,0:T(8,128)(2,1)}, u32[]{:S(2)}) copy-start(bf16[1,1,2048,384]{3,2,1,0:T(8,128)(2,1)} %param.15) | copy-start | bytes 4718596
  230.9 6.2 %copy-start.8 = (bf16[1,1,2048,384]{3,2,1,0:T(8,128)(2,1)S(1)}, bf16[1,1,2048,384]{3,2,1,0:T(8,128)(2,1)}, u32[]{:S(2)}) copy-start(bf16[1,1,2048,384]{3,2,1,0:T(8,128)(2,1)} %param.16) | copy-start | bytes 4718596
  230.9 6.2 %copy-start.9 = (bf16[1280,384]{1,0:T(8,128)(2,1)S(1)}, bf16[1280,384]{1,0:T(8,128)(2,1)}, u32[]{:S(2)}) copy-start(bf16[1280,384]{1,0:T(8,128)(2,1)} %get-tuple-element.12) | copy-start | bytes 2949124
  230.9 6.2 %copy-start.13 = (bf16[1,1,2048,384]{3,2,1,0:T(8,128)(2,1)S(1)}, bf16[1,1,2048,384]{3,2,1,0:T(8,128)(2,1)}, u32[]{:S(2)}) copy-start(bf16[1,1,2048,384]{3,2,1,0:T(8,128)(2,1)} %param.18) | copy-start | bytes 4718596
  245.5 2.7 copy-start.2
  245.5 3.1 copy-start.3
  248.7 133.9 %collective-permute-start = (bf16[3,2048,384]{2,1,0:T(8,128)(2,1)}, bf16[3,2048,384]{2,1,0:T(8,128)(2,1)}, u32[]{:S(2)}, u32[]{:S(2)}) collective-permute-start(bf16[3,2048,384]{2,1,0:T(8,128)(2,1)} %pad_maximum_fusion), channel_id=1, source_target_pairs={{0,64},{32,96},{64,0},{96,32},{1,65},{33,97},{65,1},{97,33},{2,66}... | collective-permute-start | bytes 14155784 | tf_op jit(solution)/shard_map/ppermute | solution.py:13
  248.7 133.9 %collective-permute-start.1 = (bf16[3,2048,384]{2,1,0:T(8,128)(2,1)}, bf16[3,2048,384]{2,1,0:T(8,128)(2,1)}, u32[]{:S(2)}, u32[]{:S(2)}) collective-permute-start(bf16[3,2048,384]{2,1,0:T(8,128)(2,1)} %pad_maximum_fusion), channel_id=1, source_target_pairs={{0,32},{32,0},{64,96},{96,64},{1,33},{33,1},{65,97},{97,65},{2,34}... | collective-permute-start | bytes 14155784 | tf_op jit(solution)/shard_map/ppermute | solution.py:13
  292.5 158.3 %all-to-all-start.3 = ((bf16[32,40,2048]{2,1,0:T(8,128)(2,1)}), bf16[32,40,2048]{2,1,0:T(8,128)(2,1)}, u32[]{:S(2)}, u32[]{:S(2)}) async-start(bf16[32,40,2048]{2,1,0:T(8,128)(2,1)} %bitcast.98), calls=%async_computation.3 | async-start | bytes 10485760 | tf_op jit(solution)/shard_map/all_to_all | solution.py:156
  450.8 18.1 %copy-start.1 = (bf16[128,2048]{1,0:T(8,128)(2,1)S(1)}, bf16[128,2048]{1,0:T(8,128)(2,1)}, u32[]{:S(2)}) copy-start(bf16[128,2048]{1,0:T(8,128)(2,1)} %param.11) | copy-start | bytes 1572868
where the time goes:
time: 478 us; the launch traced here: 469 us
  waiting for transfers between devices  261 us (55%)
  local copies, waits for them, and re-layouts  58 us (12%)
  matrix products  56.6 us (12%)
  other arithmetic  54.5 us (11%)
  starting transfers between devices  36.8 us (8%)
    ppermute x2, waiting for transfers between devices, partner_2(): return lax.ppermute(value, axis, pairs)  81.6 us
    all_to_all x1, waiting for transfers between devices, per_device(): lax.all_to_all(send_grad.reshape(experts, capacity, feature_width), 'expe...  57.6 us
    all_to_all x1, waiting for transfers between devices, per_device(): lax.all_to_all(send_rows.reshape(experts, capacity, feature_width), 'expe...  47.4 us
    all_to_all x1, waiting for transfers between devices, per_device(): lax.all_to_all(rows_back.reshape(experts, capacity, feature_width), 'expe...  39.1 us
    all_to_all x1, waiting for transfers between devices, per_device(): lax.all_to_all(produced.reshape(experts, capacity, feature_width), 'exper...  35.7 us
    scatter x1, local copies, waits for them, and re-layouts, per_device(): jnp.zeros((experts * capacity, feature_width), jnp.bfloat16).at[target]  23.6 us
    scatter x1, other arithmetic, per_device(): jnp.zeros((experts * capacity, feature_width), jnp.bfloat16).at[target]  23.5 us
    gather x1, local copies, waits for them, and re-layouts, per_device(): picked_back = returned_grad[target].astype(jnp.float32)  12.2 us
  transfers between devices with their start and end apart: 6, of which 5 were waited for; matrix products, arithmetic and copies ran while one was open for 22% of the time, Pallas kernels for 0%

commit v1 on v0

v1 whole, which is shorter than its diff:
```python
import jax
import jax.numpy as jnp
from jax import lax
from jax.experimental import pallas as pl
from jax.experimental.pallas import tpu as pltpu
from jax.sharding import PartitionSpec as P

momentum_beta = 0.9
learn_rate = 0.1
MESH = pl.DeviceIdType.MESH
CAP = 40
BF = jnp.bfloat16
F32 = jnp.float32
ORDER = (1, 3, 2)


def place():
    e = lax.axis_index("expert")
    return e // 16, (e // 4) % 4, e % 4


def number(xh, z, y):
    return xh * 16 + z * 4 + y


def peer(route, stage, xh, z, y, d):
    if (route == 0) == (stage == 0):
        return number(xh, z, (y + d) % 4)
    return number(xh, (z + d) % 4, y)


def greet(ids):
    barrier = pltpu.get_barrier_semaphore()
    for where in ids:
        pl.semaphore_signal(barrier, inc=1, device_id=where, device_id_type=MESH)
    pl.semaphore_wait(barrier, len(ids))


def remote(src, dst, ss, rs, where):
    return pltpu.make_async_remote_copy(
        src_ref=src, dst_ref=dst, send_sem=ss, recv_sem=rs, device_id=where, device_id_type=MESH
    )


def turn(i):
    return i + i // 2 - 2 * (i // 3)


def selection(meta, route, group):
    width = 128
    rows = lax.broadcasted_iota(jnp.int32, (2 * CAP, width), 0).astype(F32)
    first = meta[route, group, 0]
    second = meta[route, group, 1]
    hits, shares = [], []
    for e in range(4):
        hit = jnp.concatenate(
            [rows == first[e : e + 1, :], rows == second[e : e + 1, :] + float(CAP)], axis=1
        )
        share = jnp.concatenate([first[4 + e : 5 + e, :], second[4 + e : 5 + e, :]], axis=1)
        hits.append(hit)
        shares.append(jnp.where(hit, share, 0.0))
    hit = jnp.concatenate([jnp.where(h, 1.0, 0.0) for h in hits], axis=0)
    return hit, jnp.concatenate(shares, axis=0)


def dispatch_kernel(
    tok, cot, m1, m2, xo, yo, mo,
    ag, sb, xb, mr,
    ms, mrs, xs, xr, gs, gr, us, ur, ls, lo, os_,
):
    xh, z, y = place()
    half = ag.shape[-1]
    others = []
    for dx in range(2):
        for d in range(4):
            if dx or d:
                others.append({"expert": number((xh + dx) % 2, z, (y + d) % 4)})
            if d:
                others.append({"expert": number((xh + dx) % 2, (z + d) % 4, y)})
    greet(others)
    own = (y, z)
    source = (tok, cot)
    partner = {"expert": number(1 - xh, z, y)}

    def cols(a, r):
        return source[a].at[:, pl.ds(r * half, half)]

    def x_copy(a, r):
        spot = ag.at[a, r, own[r], pl.ds(xh * 128, 128)]
        return remote(cols(a, r), spot, xs.at[a, r], xr.at[a, r], partner)

    def own_copy(a, r):
        return pltpu.make_async_copy(
            cols(a, r), ag.at[a, r, own[r], pl.ds(xh * 128, 128)], ls.at[a, r]
        )

    def gather_copy(a, r, h, d):
        where = xh if h == 0 else 1 - xh
        spot = ag.at[a, r, own[r], pl.ds(where * 128, 128)]
        src = cols(a, r) if h == 0 else spot
        return remote(
            src, spot, gs.at[a, r, h, d], gr.at[a, r, h, d],
            {"expert": peer(r, 0, xh, z, y, d)},
        )

    def gather_wait(a, r, h, q):
        where = xh if h == 0 else 1 - xh
        spot = ag.at[a, r, (own[r] + q) % 4, pl.ds(where * 128, 128)]
        back = (4 - q) % 4
        remote(spot, spot, gs.at[a, r, h, back], gr.at[a, r, h, back], partner).wait_recv()

    def landing(a, r, sender, group):
        return xb.at[a, r, sender, group] if r == 0 else xb.at[a, r, group, sender]

    def spread_copy(a, r, q, d):
        group = (own[r] + q) % 4
        me = own[1 - r]
        return remote(
            sb.at[a, r, (me + d) % 4, q], landing(a, r, me, group),
            us.at[a, r, q, d], ur.at[a, r, q, d],
            {"expert": peer(r, 1, xh, z, y, d)},
        )

    def keep_copy(a, r, q):
        group = (own[r] + q) % 4
        me = own[1 - r]
        return pltpu.make_async_copy(sb.at[a, r, me, q], landing(a, r, me, group), lo.at[a, r, q])

    metas = (m1, m2)
    for r in range(2):
        mr[r, own[r], xh] = metas[r][xh, own[r]]

    def meta_copy(r, dx, d):
        to_x = (xh + dx) % 2
        to = (own[r] + d) % 4
        where = number(to_x, z, to) if r == 0 else number(to_x, to, y)
        return remote(
            metas[r].at[to_x, to], mr.at[r, own[r], xh], ms.at[r, dx, d], mrs.at[r, dx, d],
            {"expert": where},
        )

    pairs = [(dx, d) for dx in range(2) for d in range(4) if dx or d]
    for r in range(2):
        for dx, d in pairs:
            meta_copy(r, dx, d).start()
    for r in range(2):
        x_copy(0, r).start()
        own_copy(0, r).start()
    for d in ORDER:
        for r in range(2):
            gather_copy(0, r, 0, d).start()
    for r in range(2):
        x_copy(1, r).start()
        own_copy(1, r).start()

    def pass_on(a):
        for r in range(2):
            own_copy(a, r).wait()
            spot = ag.at[a, r, own[r], pl.ds((1 - xh) * 128, 128)]
            remote(spot, spot, xs.at[a, r], xr.at[a, r], partner).wait_recv()
            for d in ORDER:
                gather_copy(a, r, 1, d).start()

    pass_on(0)
    for d in ORDER:
        for r in range(2):
            gather_copy(1, r, 0, d).start()
    for r in range(2):
        for dx, d in pairs:
            meta_copy(r, dx, d).wait()

    def spread(a):
        def body(i, carry):
            q = turn(i)
            for r in range(2):
                group = (own[r] + q) % 4

                @pl.when(i > 0)
                def _():
                    gather_wait(a, r, 0, q)
                    gather_wait(a, r, 1, q)

                hit, share = selection(mr, r, group)
                hit = hit.astype(BF)
                for c in range(2):
                    part = pl.ds(c * (half // 2), half // 2)
                    rows = jnp.dot(hit, ag[a, r, group, :, part], preferred_element_type=F32)
                    if a == 1:
                        rows = rows * jnp.sum(share, axis=1, keepdims=True)
                    rows = rows.astype(BF)
                    for e in range(4):
                        sb[a, r, e, q, :, part] = rows[e * 80 : e * 80 + 80]
                for d in ORDER:
                    spread_copy(a, r, q, d).start()
                keep_copy(a, r, q).start()
            return carry

        lax.fori_loop(0, 4, body, 0)

    spread(0)
    pass_on(1)
    spread(1)
    results = (xo, yo)

    def finish(a):
        for r in range(2):
            for q in range(4):
                keep_copy(a, r, q).wait()
                for d in ORDER:
                    spread_copy(a, r, q, d).wait()
            for g in range(4):
                for k in range(4):
                    pltpu.make_async_copy(
                        xb.at[a, r, g, k],
                        results[a].at[pl.ds((g * 4 + k) * 80, 80), pl.ds(r * half, half)],
                        os_.at[a, r, g, k],
                    ).start()

    finish(0)
    finish(1)
    mo[...] = mr[...]
    for a in range(2):
        for r in range(2):
            x_copy(a, r).wait_send()
            for h in range(2):
                for d in ORDER:
                    gather_copy(a, r, h, d).wait_send()
            for g in range(4):
                for k in range(4):
                    pltpu.make_async_copy(
                        xb.at[a, r, g, k],
                        results[a].at[pl.ds((g * 4 + k) * 80, 80), pl.ds(r * half, half)],
                        os_.at[a, r, g, k],
                    ).wait()


def dispatch(tokens, cotangent, m1, m2):
    rows, width = tokens.shape
    half = width // 2
    dma = pltpu.SemaphoreType.DMA
    anywhere = pl.BlockSpec(memory_space=pl.ANY)
    vmem = pl.BlockSpec(memory_space=pltpu.VMEM)
    return pl.pallas_call(
        dispatch_kernel,
        out_shape=(
            jax.ShapeDtypeStruct((32 * CAP, width), BF),
            jax.ShapeDtypeStruct((32 * CAP, width), BF),
            jax.ShapeDtypeStruct((2, 4, 2, 8, 128), F32),
        ),
        in_specs=[anywhere, anywhere, vmem, vmem],
        out_specs=(anywhere, anywhere, vmem),
        scratch_shapes=[
            pltpu.VMEM((2, 2, 4, 256, half), BF),
            pltpu.VMEM((2, 2, 4, 4, 80, half), BF),
            pltpu.VMEM((2, 2, 4, 4, 80, half), BF),
            pltpu.VMEM((2, 4, 2, 8, 128), F32),
            dma((2, 2, 4)), dma((2, 2, 4)),
            dma((2, 2)), dma((2, 2)),
            dma((2, 2, 2, 4)), dma((2, 2, 2, 4)),
            dma((2, 2, 4, 4)), dma((2, 2, 4, 4)),
            dma((2, 2)), dma((2, 2, 4)), dma((2, 2, 4, 4)),
        ],
        compiler_params=pltpu.CompilerParams(
            collective_id=0, has_side_effects=True, vmem_limit_bytes=60 * 2**20
        ),
        name="dispatch",
    )(tokens, cotangent, m1, m2)


def combine_kernel(
    pr, bk, mr, lg, lu, ld,
    out, tg, bg0, bu0, bd0, bg1, bu1, bd1,
    rb, qs, qr, xsend, xrecv, mine,
    cs, cr, ls, ps, pt, xs, xr, ws, wr,
):
    xh, z, y = place()
    rep = lax.axis_index("replica")
    half = rb.shape[-1]
    own = (y, z)
    partner = {"expert": number(1 - xh, z, y)}
    core_mate = {"replica": rep + 1 - 2 * (rep % 2)}
    far_mate = {"replica": (rep + 2) % 4}
    others = [partner, core_mate, far_mate]
    for d in ORDER:
        others.append({"expert": number(xh, z, (y + d) % 4)})
        others.append({"expert": number(xh, (z + d) % 4, y)})
    greet(others)
    source = (pr, bk)
    results = (out, tg)

    def block(a, r, e, group):
        row = (e * 4 + group) if r == 0 else (group * 4 + e)
        return source[a].at[pl.ds(row * 80, 80), pl.ds(r * half, half)]

    def send_copy(a, r, q, d):
        group = (own[r] + q) % 4
        me = own[1 - r]
        return remote(
            block(a, r, (me + d) % 4, group), rb.at[a, r, group, me],
            cs.at[a, r, q, d], cr.at[a, r, q, d],
            {"expert": peer(r, 1, xh, z, y, d)},
        )

    def keep_copy(a, r, q):
        group = (own[r] + q) % 4
        me = own[1 - r]
        return pltpu.make_async_copy(block(a, r, me, group), rb.at[a, r, group, me], ls.at[a, r, q])

    def part_copy(a, r, q):
        return remote(
            qs.at[a, r, q], qr.at[a, r, q], ps.at[a, r, q], pt.at[a, r, q],
            {"expert": peer(r, 0, xh, z, y, q)},
        )

    def x_copy(a, r):
        return remote(xsend.at[a, r], xrecv.at[a, r], xs.at[a, r], xr.at[a, r], partner)

    weights = ((lg, bg0, bg1), (lu, bu0, bu1), (ld, bd0, bd1))
    swaps = []
    for i, (w, b0, b1) in enumerate(weights):
        swaps.append(remote(w, b1, ws.at[1, i], wr.at[1, i], far_mate))
        swaps.append(remote(w, b0, ws.at[0, i], wr.at[0, i], core_mate))
    for s in swaps:
        s.start()
    for a in range(2):
        for q in (1, 3, 2, 0):
            for r in range(2):
                keep_copy(a, r, q).start()
            for d in ORDER:
                for r in range(2):
                    send_copy(a, r, q, d).start()

    def reduce(a):
        def body(i, carry):
            q = turn((i + 1) % 4)
            for r in range(2):
                group = (own[r] + q) % 4
                keep_copy(a, r, q).wait()
                for d in ORDER:
                    send_copy(a, r, q, d).wait_recv()
                hit, share = selection(mr, r, group)
                pick = (share if a == 0 else hit).astype(BF)
                for c in range(2):
                    part = pl.ds(c * (half // 2), half // 2)
                    rows = jnp.concatenate([rb[a, r, group, e, :, part] for e in range(4)], axis=0)
                    total = lax.dot_general(
                        pick, rows, (((0,), (0,)), ((), ())), preferred_element_type=F32
                    )

                    @pl.when(i < 3)
                    def _():
                        qs[a, r, q, :, part] = total.astype(BF)

                    @pl.when(i == 3)
                    def _():
                        mine[r, :, part] = total

                @pl.when(i < 3)
                def _():
                    part_copy(a, r, q).start()
            return carry

        lax.fori_loop(0, 4, body, 0)
        there = pl.ds((1 - xh) * 128, 128)
        here = pl.ds(xh * 128, 128)
        for r in range(2):
            for q in ORDER:
                part_copy(a, r, q).wait_recv()
            away = mine[r, there]
            stay = mine[r, here]
            for q in ORDER:
                away = away + qr[a, r, q, there].astype(F32)
                stay = stay + qr[a, r, q, here].astype(F32)
            xsend[a, r] = away.astype(BF)
            x_copy(a, r).start()
            mine[2 + 2 * a + r, pl.ds(0, 128)] = stay

    reduce(0)
    reduce(1)
    for a in range(2):
        for r in range(2):
            x_copy(a, r).wait_recv()
            total = mine[2 + 2 * a + r, pl.ds(0, 128)] + xrecv[a, r].astype(F32)
            results[a][:, pl.ds(r * half, half)] = total.astype(BF)
    for a in range(2):
        for r in range(2):
            x_copy(a, r).wait_send()
            for q in range(4):
                for d in ORDER:
                    send_copy(a, r, q, d).wait_send()
            for q in ORDER:
                part_copy(a, r, q).wait_send()
    for s in swaps:
        s.wait()


def combine(produced, rows_back, meta, lg, lu, ld):
    width = produced.shape[1]
    half = width // 2
    dma = pltpu.SemaphoreType.DMA
    anywhere = pl.BlockSpec(memory_space=pl.ANY)
    vmem = pl.BlockSpec(memory_space=pltpu.VMEM)
    tokens = jax.ShapeDtypeStruct((128, width), BF)
    weights = [jax.ShapeDtypeStruct(w.shape, w.dtype) for w in (lg, lu, ld)]
    return pl.pallas_call(
        combine_kernel,
        out_shape=(tokens, tokens, *weights, *weights),
        in_specs=[anywhere, anywhere, vmem, anywhere, anywhere, anywhere],
        out_specs=(vmem, vmem, *[anywhere] * 6),
        scratch_shapes=[
            pltpu.VMEM((2, 2, 4, 4, 80, half), BF),
            pltpu.VMEM((2, 2, 4, 256, half), BF),
            pltpu.VMEM((2, 2, 4, 256, half), BF),
            pltpu.VMEM((2, 2, 128, half), BF),
            pltpu.VMEM((2, 2, 128, half), BF),
            pltpu.VMEM((6, 256, half), F32),
            dma((2, 2, 4, 4)), dma((2, 2, 4, 4)),
            dma((2, 2, 4)),
            dma((2, 2, 4)), dma((2, 2, 4)),
            dma((2, 2)), dma((2, 2)),
            dma((2, 3)), dma((2, 3)),
        ],
        compiler_params=pltpu.CompilerParams(
            collective_id=1, has_side_effects=True, vmem_limit_bytes=60 * 2**20
        ),
        name="combine",
    )(produced, rows_back, meta, lg, lu, ld)


def expert_math(rows_in, rows_grad, weight_gate, weight_up, weight_down):
    scale_in = rows_in.shape[1] ** (-0.5)
    scale_hidden = weight_gate.shape[1] ** (-0.5)
    inner = (((1,), (1,)), ((), ()))
    outer = (((0,), (0,)), ((), ()))
    gate_pre = jnp.dot(rows_in, weight_gate, preferred_element_type=F32) * scale_in
    up_pre = jnp.dot(rows_in, weight_up, preferred_element_type=F32) * scale_in
    sig = jax.nn.sigmoid(gate_pre)
    activation = (gate_pre * sig * up_pre).astype(BF)
    produced = (jnp.dot(activation, weight_down, preferred_element_type=F32) * scale_hidden).astype(BF)
    grad_act = lax.dot_general(rows_grad, weight_down, inner, preferred_element_type=F32) * scale_hidden
    grad_gate_pre = (grad_act * up_pre * sig * (1.0 + gate_pre * (1.0 - sig))).astype(BF)
    grad_up_pre = (grad_act * gate_pre * sig).astype(BF)
    grad_down = lax.dot_general(activation, rows_grad, outer, preferred_element_type=F32) * scale_hidden
    grad_gate = lax.dot_general(rows_in, grad_gate_pre, outer, preferred_element_type=F32) * scale_in
    grad_up = lax.dot_general(rows_in, grad_up_pre, outer, preferred_element_type=F32) * scale_in
    back = lax.dot_general(grad_gate_pre, weight_gate, inner, preferred_element_type=F32)
    back = back + lax.dot_general(grad_up_pre, weight_up, inner, preferred_element_type=F32)
    rows_back = (back * scale_in).astype(BF)
    return produced, rows_back, grad_gate, grad_up, grad_down


def momentum_step(weight, moment, gradient):
    moment_new = momentum_beta * moment.astype(F32) + gradient
    weight_new = (weight.astype(F32) - learn_rate * moment_new).astype(BF)
    return weight_new, moment_new.astype(BF)


def metadata(routing, gate_scores):
    share = gate_scores / jnp.sum(gate_scores, axis=1, keepdims=True)
    count = routing.shape[0]
    names = routing.T[:, None, :] == jnp.arange(32, dtype=jnp.int32)[None, :, None]
    member = jnp.any(names, axis=0)
    shares = jnp.sum(jnp.where(names, share.T[:, None, :], 0.0), axis=0)
    spot = jnp.arange(count, dtype=jnp.int32)
    before = (spot[:, None] < spot[None, :]).astype(BF)
    earlier = jnp.dot(member.astype(BF), before, preferred_element_type=F32)
    slots = jnp.where(member, earlier, -1000.0).reshape(2, 4, 4, count)
    shares = shares.reshape(2, 4, 4, count)
    m2 = jnp.concatenate([slots, shares], axis=2)
    m1 = jnp.concatenate([slots.transpose(0, 2, 1, 3), shares.transpose(0, 2, 1, 3)], axis=2)
    return m1, m2


def per_device(
    tokens, routing, gate_scores, cotangent,
    w_gate, w_up, w_down, mom_gate, mom_up, mom_down, gossip_round,
):
    m1, m2 = metadata(routing, gate_scores)
    rows_in, rows_grad, meta = dispatch(tokens, cotangent, m1, m2)
    weight_gate, weight_up, weight_down = w_gate[0, 0], w_up[0, 0], w_down[0, 0]
    produced, rows_back, grad_gate, grad_up, grad_down = expert_math(
        rows_in, rows_grad, weight_gate, weight_up, weight_down
    )
    gate_new, gate_moment = momentum_step(weight_gate, mom_gate[0, 0], grad_gate)
    up_new, up_moment = momentum_step(weight_up, mom_up[0, 0], grad_up)
    down_new, down_moment = momentum_step(weight_down, mom_down[0, 0], grad_down)
    layer_out, token_grad, *swapped = combine(
        produced, rows_back, meta, gate_new, up_new, down_new
    )
    near = gossip_round[0] % 2 == 0
    averaged = []
    for i, local in enumerate((gate_new, up_new, down_new)):
        other = jnp.where(near, swapped[i].astype(F32), swapped[3 + i].astype(F32))
        averaged.append(((local.astype(F32) + other) * 0.5).astype(BF)[None, None])
    return (
        layer_out, token_grad, *averaged,
        gate_moment[None, None], up_moment[None, None], down_moment[None, None],
    )


def solution(mesh):
    flat = P(("replica", "expert"), None)
    stacked = P("replica", "expert", None, None)
    return jax.shard_map(
        per_device,
        mesh=mesh,
        in_specs=(flat,) * 4 + (stacked,) * 6 + (P("expert"),),
        out_specs=(flat,) * 2 + (stacked,) * 6,
        check_vma=False,
    )
```

time: 478 us -> 314 us (0.66)
  waiting for transfers between devices: 261 us -> 0 us
  Pallas kernels: 0 us -> 247 us
  local copies, waits for them, and re-layouts: 58 us -> 2.28 us
  other arithmetic: 54.5 us -> 12.6 us
  starting transfers between devices: 36.8 us -> 0 us
  matrix products: 56.6 us -> 45.7 us
    pallas_call x0 -> x2, Pallas kernels: none -> 247 us  [the longest x1 131 us: combine(): pl.pallas_call(combine_kernel, out_shape=(tokens, tokens, *weights, *weig...]
    all_to_all x4 -> x0, waiting for transfers between devices: 180 us -> none  [the longest x1 57.6 us: per_device(): lax.all_to_all(send_grad.reshape(experts, capacity, feature_width), 'expe...]
    ppermute x2 -> x0, waiting for transfers between devices: 81.6 us -> none  [partner_2(): return lax.ppermute(value, axis, pairs)]
    all_to_all x4 -> x0, starting transfers between devices: 36.4 us -> none  [the longest x1 9.73 us: per_device(): lax.all_to_all(send_rows.reshape(experts, capacity, feature_width), 'expe...]
    gather x2 -> x0, local copies, waits for them, and re-layouts: 24.2 us -> none  [the longest x1 12.2 us: per_device(): picked_back = returned_grad[target].astype(jnp.float32)]
    scatter x1 -> x0, local copies, waits for them, and re-layouts: 23.6 us -> none  [per_device(): jnp.zeros((experts * capacity, feature_width), jnp.bfloat16).at[target]]
    scatter x1 -> x0, other arithmetic: 23.5 us -> none  [per_device(): jnp.zeros((experts * capacity, feature_width), jnp.bfloat16).at[target]]
    reduce_sum x4 -> x2, other arithmetic: 13.3 us -> 1.42 us  [the longest x1 0.71 us: metadata(): shares = jnp.sum(jnp.where(names, share.T[:, None, :], 0.0), axis=0)]
  transfers between devices with their start and end apart: 6 -> 0, of which waited for: 5 -> 0; matrix products, arithmetic and copies ran while one was open for 22% -> 0% of each run, Pallas kernels for 0% -> 0%
where the time goes in v1:
time: 314 us; the launch traced here: 309 us
  Pallas kernels  247 us (79%)
  matrix products  45.7 us (15%)
  other arithmetic  12.6 us (4%)
    pallas_call x1, Pallas kernels, combine(): pl.pallas_call(combine_kernel, out_shape=(tokens, tokens, *weights, *weig...  131 us
    pallas_call x1, Pallas kernels, dispatch(): pl.pallas_call(dispatch_kernel, out_shape=(jax.ShapeDtypeStruct((32 * CAP...  116 us
    broadcast_in_dim x2, other arithmetic, per_device(): averaged.append(((local.astype(F32) + other) * 0.5).astype(BF)[None, None])  9.15 us
    dot_general x1, matrix products, expert_math(): lax.dot_general(rows_in, grad_up_pre, outer, preferred_element_type=F32)  8.35 us
    dot_general x1, matrix products, expert_math(): lax.dot_general(rows_in, grad_gate_pre, outer, preferred_element_type=F32)  7.9 us

profile of v1, /device:TPU:50, one launch (start us, length us, event | category | flops | bytes accessed | tf_op | source)
XLA Modules:
  0.0 309.4 jit_solution(14684772564769741307)
XLA Ops:
  0.6 0.7 reduce_sum.18
  1.3 0.7 divide_bitcast_fusion
  2.0 0.7 select_reduce_fusion
  2.7 0.7 fusion.10
  3.5 0.1 convolution_select_fusion
  3.6 0.6 copy.20.m1
  4.2 0.6 pad_maximum_fusion.1.m2
  4.8 116.1 %dispatch.1 = (bf16[1280,2048]{1,0:T(8,128)(2,1)}, bf16[1280,2048]{1,0:T(8,128)(2,1)}, f32[2,4,2,8,128]{4,3,2,1,0:T(8,128)}) custom-call(bf16[128,2048]{1,0:T(8,128)(2,1)} %tok.1, bf16[128,2048]{1,0:T(8,128)(2,1)} %cot.1, f32[2,4,8,128]{3,2,1,0:T(8,128)} %copy.20.m1, f32[2,4,8,128]{3,2,1,0:T(8,128)} %pad_maximum_fusion.1.m2), custom_call_target="tpu_custom_call" | custom-call | tf_op jit(solution)/shard_map/dispatch/pallas_call | solution.py:243
  121.0 0.0 copy-start.4
  121.0 0.0 slice-start
  121.0 5.4 %convolution_multiply_fusion.1 = f32[1280,384]{1,0:T(8,128)S(1)} fusion(bf16[1280,2048]{1,0:T(8,128)(2,1)} %get-tuple-element.19, bf16[1,1,2048,384]{3,2,1,0:T(8,128)(2,1)} %param.16), kind=kOutput, calls=%fused_computation.12 | convolution fusion | flops 2013757440 | bytes 8781824 | tf_op jit(solution)/shard_map/dot_general | solution.py:436
  126.4 0.0 copy-done.4
  126.4 0.0 copy-done.11
  126.4 0.0 slice-start.1
  126.5 0.0 copy-start.6
  126.5 2.9 convolution_multiply_fusion.2
  129.4 0.0 slice-done
  129.4 3.8 %multiply_convert_fusion.5 = (bf16[1280,384]{1,0:T(8,128)(2,1)S(1)}, bf16[1280,384]{1,0:T(8,128)(2,1)S(1)}, bf16[1280,384]{1,0:T(8,128)(2,1)S(1)}) fusion(f32[1280,384]{1,0:T(8,128)S(1)} %convolution_multiply_fusion.2, f32[1280,384]{1,0:T(8,128)S(1)} %convolution_multiply_fusion.1, bf16[1280,2048]{1,0:T(8,128)(2,1)S(1)} %bitcast.71, ...), kind=kOutput, calls=%fused_computation.14 | convolution fusion | flops 2021621760 | bytes 13697024 | tf_op jit(solution)/shard_map/dot_general | solution.py:440
  133.3 0.0 copy-start.3
  133.3 2.9 fusion.7
  136.2 5.0 %multiply_convert_fusion.bk = bf16[1280,2048]{1,0:T(8,128)(2,1)} fusion(f32[1280,2048]{1,0:T(8,128)S(1)} %fusion.7, bf16[1280,384]{1,0:T(8,128)(2,1)S(1)} %get-tuple-element.30, bf16[1,1,2048,384]{3,2,1,0:T(8,128)(2,1)S(1)} %copy-done.3), kind=kOutput, calls=%fused_computation | convolution fusion | flops 2021130240 | bytes 18284544 | tf_op jit(solution)/shard_map/dot_general | solution.py:447
  141.2 8.4 %convert_bitcast_fusion.1 = (bf16[1,1,2048,384]{3,2,1,0:T(8,128)(2,1)}, bf16[2048,384]{1,0:T(8,128)(2,1)}) fusion(bf16[1,1,2048,384]{3,2,1,0:T(8,128)(2,1)S(1)} %copy-done.3, bf16[1280,2048]{1,0:T(8,128)(2,1)} %get-tuple-element.19, bf16[1280,384]{1,0:T(8,128)(2,1)S(1)} %get-tuple-element.30, bf16[1,1,2048,384]{3,2,1,0:T(8,128)(2,1)} %param.19), kind=kOutput, calls=%fused_computation.29 | convolution fusion | flops 2020343808 | bytes 12517376 | tf_op jit(solution)/shard_map/dot_general | solution.py:445
  149.5 7.9 %convert_bitcast_fusion.2 = (bf16[1,1,2048,384]{3,2,1,0:T(8,128)(2,1)}, bf16[2048,384]{1,0:T(8,128)(2,1)}) fusion(bf16[1,1,2048,384]{3,2,1,0:T(8,128)(2,1)S(1)} %copy-done.4, bf16[1280,2048]{1,0:T(8,128)(2,1)} %get-tuple-element.19, bf16[1280,384]{1,0:T(8,128)(2,1)S(1)} %get-tuple-element.31, bf16[1,1,2048,384]{3,2,1,0:T(8,128)(2,1)S(1)} %copy-done.12), kind=kOutput, calls=%fused_computation.30 | convolution fusion | flops 2020343808 | bytes 12517376 | tf_op jit(solution)/shard_map/dot_general | solution.py:444
  157.5 4.6 %convert_bitcast_fusion = (bf16[1,1,384,2048]{3,2,1,0:T(8,128)(2,1)}, bf16[384,2048]{1,0:T(8,128)(2,1)}) fusion(bf16[1,1,384,2048]{3,2,1,0:T(8,128)(2,1)S(1)} %copy-done.6, bf16[1280,384]{1,0:T(8,128)(2,1)S(1)} %get-tuple-element.32, bf16[1280,2048]{1,0:T(8,128)(2,1)S(1)} %bitcast.71, bf16[1,1,384,2048]{3,2,1,0:T(8,128)(2,1)S(1)} %copy-done.5), kind=kOutput, calls=%fused_computation.28 | convolution fusion | flops 2020343808 | bytes 12517376 | tf_op jit(solution)/shard_map/dot_general | solution.py:443
  162.1 4.6 %multiply_convert_fusion.1.pr = bf16[1280,2048]{1,0:T(8,128)(2,1)} fusion(bf16[1280,384]{1,0:T(8,128)(2,1)S(1)} %get-tuple-element.32, bf16[1,1,384,2048]{3,2,1,0:T(8,128)(2,1)S(1)} %copy-done.6), kind=kOutput, calls=%fused_computation.1 | convolution fusion | flops 2018508800 | bytes 7798784 | tf_op jit(solution)/shard_map/dot_general | solution.py:439
  166.7 131.2 %combine.1 = (bf16[128,2048]{1,0:T(8,128)(2,1)}, bf16[128,2048]{1,0:T(8,128)(2,1)}, bf16[2048,384]{1,0:T(8,128)(2,1)}, bf16[2048,384]{1,0:T(8,128)(2,1)}, bf16[3...) custom-call(bf16[1280,2048]{1,0:T(8,128)(2,1)} %multiply_convert_fusion., ...), custom_call_target="tpu_custom_call" | custom-call | tf_op jit(solution)/shard_map/combine/pallas_call | solution.py:405
  298.5 0.0 copy-start.1
  298.5 0.0 copy-start.2
  298.6 4.0 %fusion.2 = bf16[1,1,384,2048]{3,2,1,0:T(8,128)(2,1)} fusion(bf16[384,2048]{1,0:T(8,128)(2,1)} %get-tuple-element.29, bf16[384,2048]{1,0:T(8,128)(2,1)} %get-tuple-element.28, bf16[384,2048]{1,0:T(8,128)(2,1)S(1)} %copy-done, pred[]{:T(512)S(6)} %eq.21), kind=kLoop, calls=%fused_computation.20 | loop fusion | flops 5505024 | bytes 6291457 | tf_op jit(solution)/shard_map/broadcast_in_dim | solution.py:494
  302.7 5.1 %fusion = (bf16[1,1,2048,384]{3,2,1,0:T(8,128)(2,1)}, bf16[1,1,2048,384]{3,2,1,0:T(8,128)(2,1)}) fusion(bf16[2048,384]{1,0:T(8,128)(2,1)} %get-tuple-element.25, bf16[2048,384]{1,0:T(8,128)(2,1)S(1)} %copy-done.7, bf16[2048,384]{1,0:T(8,128)(2,1)S(1)} %copy-done.2, pred[]{:T(512)S(6)} %eq.21, bf16[2048,384]{1,0:T(8,128)(2,1)} %get-tuple-element.27, ...), kind=kLoop, calls=%fused_computation.18 | loop fusion | flops 11010048 | bytes 12582913 | tf_op jit(solution)/shard_map/broadcast_in_dim | solution.py:494
  307.8 0.8 copy.24
  308.6 0.8 copy.25
  (22 shorter events, 0.1 us)
Async XLA Ops:
  121.0 5.5 %copy-start.4 = (bf16[1,1,2048,384]{3,2,1,0:T(8,128)(2,1)S(1)}, bf16[1,1,2048,384]{3,2,1,0:T(8,128)(2,1)}, u32[]{:S(2)}) copy-start(bf16[1,1,2048,384]{3,2,1,0:T(8,128)(2,1)} %param.15) | copy-start | bytes 4718596
  121.0 5.5 %copy-start.11 = (bf16[1280,2048]{1,0:T(8,128)(2,1)S(1)}, bf16[1280,2048]{1,0:T(8,128)(2,1)}, u32[]{:S(2)}) copy-start(bf16[1280,2048]{1,0:T(8,128)(2,1)} %get-tuple-element.19) | copy-start | bytes 15728644
  121.0 8.4 %slice-start = ((s8[5242880]{0:T(1024)(128)(4,1)}), s8[4194304]{0:T(1024)(128)(4,1)S(1)}, s32[]{:S(2)}) async-start(s8[5242880]{0:T(1024)(128)(4,1)} %bitcast.70), calls=%async_computation | async-start | bytes 8388608
  126.4 3.0 slice-start.1
  126.5 3.0 copy-start.6
  133.3 2.9 copy-start.3
  141.2 8.4 %copy-start.12 = (bf16[1,1,2048,384]{3,2,1,0:T(8,128)(2,1)S(1)}, bf16[1,1,2048,384]{3,2,1,0:T(8,128)(2,1)}, u32[]{:S(2)}) copy-start(bf16[1,1,2048,384]{3,2,1,0:T(8,128)(2,1)} %param.18) | copy-start | bytes 4718596
  149.5 7.9 %copy-start.5 = (bf16[1,1,384,2048]{3,2,1,0:T(8,128)(2,1)S(1)}, bf16[1,1,384,2048]{3,2,1,0:T(8,128)(2,1)}, u32[]{:S(2)}) copy-start(bf16[1,1,384,2048]{3,2,1,0:T(8,128)(2,1)} %param.20) | copy-start | bytes 4718596
  166.7 131.8 %copy-start = (bf16[384,2048]{1,0:T(8,128)(2,1)S(1)}, bf16[384,2048]{1,0:T(8,128)(2,1)}, u32[]{:S(2)}) copy-start(bf16[384,2048]{1,0:T(8,128)(2,1)} %get-tuple-element.34.ld) | copy-start | bytes 4718596
  298.5 4.1 %copy-start.1 = (bf16[2048,384]{1,0:T(8,128)(2,1)S(1)}, bf16[2048,384]{1,0:T(8,128)(2,1)}, u32[]{:S(2)}) copy-start(bf16[2048,384]{1,0:T(8,128)(2,1)} %get-tuple-element.36.lu) | copy-start | bytes 4718596
  298.5 4.1 %copy-start.2 = (bf16[2048,384]{1,0:T(8,128)(2,1)S(1)}, bf16[2048,384]{1,0:T(8,128)(2,1)}, u32[]{:S(2)}) copy-start(bf16[2048,384]{1,0:T(8,128)(2,1)} %get-tuple-element.38.lg) | copy-start | bytes 4718596
  298.6 4.1 %copy-start.7 = (bf16[2048,384]{1,0:T(8,128)(2,1)S(1)}, bf16[2048,384]{1,0:T(8,128)(2,1)}, u32[]{:S(2)}) copy-start(bf16[2048,384]{1,0:T(8,128)(2,1)} %get-tuple-element.24) | copy-start | bytes 4718596
  298.6 4.1 %copy-start.8 = (bf16[2048,384]{1,0:T(8,128)(2,1)S(1)}, bf16[2048,384]{1,0:T(8,128)(2,1)}, u32[]{:S(2)}) copy-start(bf16[2048,384]{1,0:T(8,128)(2,1)} %get-tuple-element.26) | copy-start | bytes 4718596
  302.6 5.1 %copy-start.10 = (bf16[128,2048]{1,0:T(8,128)(2,1)S(1)}, bf16[128,2048]{1,0:T(8,128)(2,1)}, u32[]{:S(2)}) copy-start(bf16[128,2048]{1,0:T(8,128)(2,1)} %get-tuple-element.49) | copy-start | bytes 1572868
  302.7 5.9 %copy-start.9 = (bf16[128,2048]{1,0:T(8,128)(2,1)S(1)}, bf16[128,2048]{1,0:T(8,128)(2,1)}, u32[]{:S(2)}) copy-start(bf16[128,2048]{1,0:T(8,128)(2,1)} %get-tuple-element.50) | copy-start | bytes 1572868

commit v2 on v1

v2 whole, which is shorter than its diff:
```python
import jax
import jax.numpy as jnp
from jax import lax
from jax.experimental import pallas as pl
from jax.experimental.pallas import tpu as pltpu
from jax.sharding import PartitionSpec as P

momentum_beta = 0.9
learn_rate = 0.1
MESH = pl.DeviceIdType.MESH
CAP = 40
BF = jnp.bfloat16
F32 = jnp.float32
ORDER = (1, 3, 2)


def place():
    e = lax.axis_index("expert")
    return e // 16, (e // 4) % 4, e % 4


def number(xh, z, y):
    return xh * 16 + z * 4 + y


def peer(route, stage, xh, z, y, d):
    if (route == 0) == (stage == 0):
        return number(xh, z, (y + d) % 4)
    return number(xh, (z + d) % 4, y)


def greet(ids):
    barrier = pltpu.get_barrier_semaphore()
    for where in ids:
        pl.semaphore_signal(barrier, inc=1, device_id=where, device_id_type=MESH)
    pl.semaphore_wait(barrier, len(ids))


def remote(src, dst, ss, rs, where):
    return pltpu.make_async_remote_copy(
        src_ref=src, dst_ref=dst, send_sem=ss, recv_sem=rs, device_id=where, device_id_type=MESH
    )


def turn(i):
    return i + i // 2 - 2 * (i // 3)


def selection(meta, route, group):
    width = 128
    rows = lax.broadcasted_iota(jnp.int32, (2 * CAP, width), 0).astype(F32)
    first = meta[route, group, 0]
    second = meta[route, group, 1]
    hits, shares = [], []
    for e in range(4):
        hit = jnp.concatenate(
            [rows == first[e : e + 1, :], rows == second[e : e + 1, :] + float(CAP)], axis=1
        )
        share = jnp.concatenate([first[4 + e : 5 + e, :], second[4 + e : 5 + e, :]], axis=1)
        hits.append(hit)
        shares.append(jnp.where(hit, share, 0.0))
    hit = jnp.concatenate([jnp.where(h, 1.0, 0.0) for h in hits], axis=0)
    return hit, jnp.concatenate(shares, axis=0)


def metadata(rt, gt, m1, m2):
    share = gt[...] / jnp.sum(gt[...], axis=0, keepdims=True)
    names = lax.broadcasted_iota(jnp.int32, (32, 128), 0)
    member = jnp.zeros((32, 128), F32)
    shares = jnp.zeros((32, 128), F32)
    for k in range(8):
        same = rt[k : k + 1, :] == names
        member = member + jnp.where(same, 1.0, 0.0)
        shares = shares + jnp.where(same, share[k : k + 1, :], 0.0)
    earlier_token = lax.broadcasted_iota(jnp.int32, (128, 128), 0)
    later_token = lax.broadcasted_iota(jnp.int32, (128, 128), 1)
    before = jnp.where(earlier_token < later_token, 1.0, 0.0).astype(BF)
    earlier = jnp.dot(member.astype(BF), before, preferred_element_type=F32)
    slots = jnp.where(member > 0.0, earlier, -1000.0)
    for xh in range(2):
        for i in range(4):
            for k in range(4):
                e1 = xh * 16 + k * 4 + i
                e2 = xh * 16 + i * 4 + k
                m1[xh, i, k : k + 1, :] = slots[e1 : e1 + 1]
                m1[xh, i, 4 + k : 5 + k, :] = shares[e1 : e1 + 1]
                m2[xh, i, k : k + 1, :] = slots[e2 : e2 + 1]
                m2[xh, i, 4 + k : 5 + k, :] = shares[e2 : e2 + 1]


def dispatch_kernel(
    tok, cot, rt, gt, wg, wu, wd,
    xo, yo, po, guo, aco, mo,
    ag, sb, xb, mr, m1, m2, wgu, wdn, gus, acs, prs,
    ms, mrs, xs, xr, gs, gr, us, ur, ls, lo, os_, wl, fo,
):
    xh, z, y = place()
    half = ag.shape[-1]
    hidden = wd.shape[0]
    scale_in = (2 * half) ** (-0.5)
    scale_hidden = hidden ** (-0.5)
    loads = [
        pltpu.make_async_copy(wg, wgu.at[:, pl.ds(0, hidden)], wl.at[0]),
        pltpu.make_async_copy(wu, wgu.at[:, pl.ds(hidden, hidden)], wl.at[1]),
        pltpu.make_async_copy(wd, wdn, wl.at[2]),
    ]
    others = []
    for dx in range(2):
        for d in range(4):
            if dx or d:
                others.append({"expert": number((xh + dx) % 2, z, (y + d) % 4)})
            if d:
                others.append({"expert": number((xh + dx) % 2, (z + d) % 4, y)})
    greet(others)
    own = (y, z)
    source = (tok, cot)
    partner = {"expert": number(1 - xh, z, y)}

    def cols(a, r):
        return source[a].at[:, pl.ds(r * half, half)]

    def x_copy(a, r):
        spot = ag.at[a, r, own[r], pl.ds(xh * 128, 128)]
        return remote(cols(a, r), spot, xs.at[a, r], xr.at[a, r], partner)

    def own_copy(a, r):
        return pltpu.make_async_copy(
            cols(a, r), ag.at[a, r, own[r], pl.ds(xh * 128, 128)], ls.at[a, r]
        )

    def gather_copy(a, r, h, d):
        where = xh if h == 0 else 1 - xh
        spot = ag.at[a, r, own[r], pl.ds(where * 128, 128)]
        src = cols(a, r) if h == 0 else spot
        return remote(
            src, spot, gs.at[a, r, h, d], gr.at[a, r, h, d],
            {"expert": peer(r, 0, xh, z, y, d)},
        )

    def gather_wait(a, r, h, q):
        where = xh if h == 0 else 1 - xh
        spot = ag.at[a, r, (own[r] + q) % 4, pl.ds(where * 128, 128)]
        back = (4 - q) % 4
        remote(spot, spot, gs.at[a, r, h, back], gr.at[a, r, h, back], partner).wait_recv()

    def landing(a, r, sender, group):
        row = (sender * 4 + group) if r == 0 else (group * 4 + sender)
        return xb.at[a, r, pl.ds(row * 80, 80)]

    def spread_copy(a, r, q, d):
        group = (own[r] + q) % 4
        me = own[1 - r]
        return remote(
            sb.at[a, r, (me + d) % 4, q], landing(a, r, me, group),
            us.at[a, r, q, d], ur.at[a, r, q, d],
            {"expert": peer(r, 1, xh, z, y, d)},
        )

    def keep_copy(a, r, q):
        group = (own[r] + q) % 4
        me = own[1 - r]
        return pltpu.make_async_copy(sb.at[a, r, me, q], landing(a, r, me, group), lo.at[a, r, q])

    metas = (m1, m2)

    def meta_copy(r, dx, d):
        to_x = (xh + dx) % 2
        to = (own[r] + d) % 4
        where = number(to_x, z, to) if r == 0 else number(to_x, to, y)
        return remote(
            metas[r].at[to_x, to], mr.at[r, own[r], xh], ms.at[r, dx, d], mrs.at[r, dx, d],
            {"expert": where},
        )

    for r in range(2):
        x_copy(0, r).start()
        own_copy(0, r).start()
    for d in ORDER:
        for r in range(2):
            gather_copy(0, r, 0, d).start()
    for r in range(2):
        x_copy(1, r).start()
        own_copy(1, r).start()
    for load in loads:
        load.start()
    pairs = [(dx, d) for dx in range(2) for d in range(4) if dx or d]
    metadata(rt, gt, m1, m2)
    for r in range(2):
        mr[r, own[r], xh] = metas[r][xh, own[r]]
    for r in range(2):
        for dx, d in pairs:
            meta_copy(r, dx, d).start()

    def pass_on(a):
        for r in range(2):
            own_copy(a, r).wait()
            spot = ag.at[a, r, own[r], pl.ds((1 - xh) * 128, 128)]
            remote(spot, spot, xs.at[a, r], xr.at[a, r], partner).wait_recv()
            for d in ORDER:
                gather_copy(a, r, 1, d).start()

    pass_on(0)
    for d in ORDER:
        for r in range(2):
            gather_copy(1, r, 0, d).start()
    for r in range(2):
        for dx, d in pairs:
            meta_copy(r, dx, d).wait()

    def spread(a):
        def body(i, carry):
            q = turn(i)
            for r in range(2):
                group = (own[r] + q) % 4

                @pl.when(i > 0)
                def _():
                    gather_wait(a, r, 0, q)
                    gather_wait(a, r, 1, q)

                hit, share = selection(mr, r, group)
                hit = hit.astype(BF)
                for c in range(2):
                    part = pl.ds(c * (half // 2), half // 2)
                    rows = jnp.dot(hit, ag[a, r, group, :, part], preferred_element_type=F32)
                    if a == 1:
                        rows = rows * jnp.sum(share, axis=1, keepdims=True)
                    rows = rows.astype(BF)
                    for e in range(4):
                        sb[a, r, e, q, :, part] = rows[e * 80 : e * 80 + 80]
                for d in ORDER:
                    spread_copy(a, r, q, d).start()
                keep_copy(a, r, q).start()
            return carry

        lax.fori_loop(0, 4, body, 0)

    spread(0)
    pass_on(1)
    spread(1)
    results = (xo, yo)

    def arrive(a):
        for r in range(2):
            for q in range(4):
                keep_copy(a, r, q).wait()
                for d in ORDER:
                    spread_copy(a, r, q, d).wait()
            pltpu.make_async_copy(xb.at[a, r], results[a].at[r], os_.at[a, r]).start()

    arrive(0)
    for load in loads:
        load.wait()

    def stores(t):
        part = pl.ds(t * 320, 320)
        found = [
            pltpu.make_async_copy(gus.at[part], guo.at[part], fo.at[t, 0]),
            pltpu.make_async_copy(acs.at[part], aco.at[part], fo.at[t, 1]),
        ]
        for r in range(2):
            found.append(pltpu.make_async_copy(prs.at[r, part], po.at[r, part], fo.at[t, 2 + r]))
        return found

    def forward(t, carry):
        part = pl.ds(t * 320, 320)
        both = jnp.dot(xb[0, 0, part], wgu[pl.ds(0, half)], preferred_element_type=F32)
        both = both + jnp.dot(xb[0, 1, part], wgu[pl.ds(half, half)], preferred_element_type=F32)
        both = both * scale_in
        gus[part] = both
        gate = both[:, :hidden]
        act = (gate * jax.nn.sigmoid(gate) * both[:, hidden:]).astype(BF)
        acs[part] = act
        for r in range(2):
            made = jnp.dot(act, wdn[:, pl.ds(r * half, half)], preferred_element_type=F32)
            prs[r, part] = (made * scale_hidden).astype(BF)
        for s in stores(t):
            s.start()
        return carry

    lax.fori_loop(0, 4, forward, 0)
    arrive(1)
    mo[...] = mr[...]
    for t in range(4):
        for s in stores(t):
            s.wait()
    for a in range(2):
        for r in range(2):
            x_copy(a, r).wait_send()
            for h in range(2):
                for d in ORDER:
                    gather_copy(a, r, h, d).wait_send()
            pltpu.make_async_copy(xb.at[a, r], results[a].at[r], os_.at[a, r]).wait()


def dispatch(tokens, cotangent, rt, gt, wg, wu, wd):
    rows, width = tokens.shape
    half = width // 2
    hidden = wd.shape[0]
    dma = pltpu.SemaphoreType.DMA
    anywhere = pl.BlockSpec(memory_space=pl.ANY)
    vmem = pl.BlockSpec(memory_space=pltpu.VMEM)
    slots = 32 * CAP
    halves = jax.ShapeDtypeStruct((2, slots, half), BF)
    return pl.pallas_call(
        dispatch_kernel,
        out_shape=(
            halves, halves, halves,
            jax.ShapeDtypeStruct((slots, 2 * hidden), F32),
            jax.ShapeDtypeStruct((slots, hidden), BF),
            jax.ShapeDtypeStruct((2, 4, 2, 8, 128), F32),
        ),
        in_specs=[anywhere, anywhere, vmem, vmem, anywhere, anywhere, anywhere],
        out_specs=(*[anywhere] * 5, vmem),
        scratch_shapes=[
            pltpu.VMEM((2, 2, 4, 256, half), BF),
            pltpu.VMEM((2, 2, 4, 4, 80, half), BF),
            pltpu.VMEM((2, 2, slots, half), BF),
            pltpu.VMEM((2, 4, 2, 8, 128), F32),
            pltpu.VMEM((2, 4, 8, 128), F32),
            pltpu.VMEM((2, 4, 8, 128), F32),
            pltpu.VMEM((width, 2 * hidden), BF),
            pltpu.VMEM((hidden, width), BF),
            pltpu.VMEM((slots, 2 * hidden), F32),
            pltpu.VMEM((slots, hidden), BF),
            pltpu.VMEM((2, slots, half), BF),
            dma((2, 2, 4)), dma((2, 2, 4)),
            dma((2, 2)), dma((2, 2)),
            dma((2, 2, 2, 4)), dma((2, 2, 2, 4)),
            dma((2, 2, 4, 4)), dma((2, 2, 4, 4)),
            dma((2, 2)), dma((2, 2, 4)), dma((2, 2)),
            dma((3,)), dma((4, 4)),
        ],
        compiler_params=pltpu.CompilerParams(
            collective_id=0, has_side_effects=True, vmem_limit_bytes=60 * 2**20
        ),
        name="dispatch",
    )(tokens, cotangent, rt, gt, wg, wu, wd)


def combine_kernel(
    xi, yi, pr, gui, aci, mr, wg, wu, wd, mg, mu, md,
    out, tg, lgu_o, ld_o, mgu_o, md_o, bgu, bd,
    xv, yv, gup, acv, grads, wgu, wdn, mgu, mdn, lgu, ldn,
    rb, qs, qr, xsend, xrecv, mine, kept,
    cs, cr, ls, ps, pt, xs, xr, ws, wr, wl, go,
):
    xh, z, y = place()
    rep = lax.axis_index("replica")
    half = rb.shape[-1]
    hidden = wd.shape[0]
    scale_in = (2 * half) ** (-0.5)
    scale_hidden = hidden ** (-0.5)
    low, high = pl.ds(0, hidden), pl.ds(hidden, hidden)
    copies = [
        (wd, wdn), (yi, yv), (gui, gup), (xi, xv), (wg, wgu.at[:, low]), (wu, wgu.at[:, high]),
        (mg, mgu.at[:, low]), (mu, mgu.at[:, high]), (aci, acv), (md, mdn),
    ]
    loads = [pltpu.make_async_copy(s, d, wl.at[i]) for i, (s, d) in enumerate(copies)]
    for load in loads:
        load.start()
    own = (y, z)
    partner = {"expert": number(1 - xh, z, y)}
    core_mate = {"replica": rep + 1 - 2 * (rep % 2)}
    far_mate = {"replica": (rep + 2) % 4}
    others = [partner, core_mate, far_mate]
    for d in ORDER:
        others.append({"expert": number(xh, z, (y + d) % 4)})
        others.append({"expert": number(xh, (z + d) % 4, y)})
    greet(others)
    source = (pr, xv)
    results = (out, tg)

    def block(a, r, e, group):
        row = (e * 4 + group) if r == 0 else (group * 4 + e)
        return source[a].at[r, pl.ds(row * 80, 80)]

    def send_copy(a, r, q, d):
        group = (own[r] + q) % 4
        me = own[1 - r]
        return remote(
            block(a, r, (me + d) % 4, group), rb.at[a, r, group, me],
            cs.at[a, r, q, d], cr.at[a, r, q, d],
            {"expert": peer(r, 1, xh, z, y, d)},
        )

    def keep_copy(a, r, q):
        group = (own[r] + q) % 4
        me = own[1 - r]
        return pltpu.make_async_copy(block(a, r, me, group), rb.at[a, r, group, me], ls.at[a, r, q])

    def part_copy(a, r, q):
        return remote(
            qs.at[a, r, q - 1], qr.at[a, r, q - 1], ps.at[a, r, q], pt.at[a, r, q],
            {"expert": peer(r, 0, xh, z, y, q)},
        )

    def x_copy(a, r):
        return remote(xsend.at[a, r], xrecv.at[a, r], xs.at[a, r], xr.at[a, r], partner)

    def send_rows(a):
        for q in (1, 3, 2, 0):
            for r in range(2):
                keep_copy(a, r, q).start()
            for d in ORDER:
                for r in range(2):
                    send_copy(a, r, q, d).start()

    def in_tile(t):
        rows = pl.ds(t * 256, 256)
        src = lgu.at[rows]
        return [
            remote(src, bgu.at[1, rows], ws.at[1, t], wr.at[1, t], far_mate),
            remote(src, bgu.at[0, rows], ws.at[0, t], wr.at[0, t], core_mate),
        ]

    def down_tile(c):
        cols = pl.ds(c * 512, 512)
        src = ldn.at[:, cols]
        return [
            remote(src, bd.at[1, :, cols], ws.at[1, 8 + c], wr.at[1, 8 + c], far_mate),
            remote(src, bd.at[0, :, cols], ws.at[0, 8 + c], wr.at[0, 8 + c], core_mate),
        ]

    send_rows(0)
    for load in loads[:3]:
        load.wait()

    def hidden_grads(t, carry):
        part = pl.ds(t * 320, 320)
        inner = (((1,), (1,)), ((), ()))
        grad_act = lax.dot_general(
            yv[0, part], wdn[:, pl.ds(0, half)], inner, preferred_element_type=F32
        )
        grad_act = grad_act + lax.dot_general(
            yv[1, part], wdn[:, pl.ds(half, half)], inner, preferred_element_type=F32
        )
        grad_act = grad_act * scale_hidden
        gate = gup[part, low]
        up = gup[part, high]
        sig = jax.nn.sigmoid(gate)
        grads[part, low] = (grad_act * up * sig * (1.0 + gate * (1.0 - sig))).astype(BF)
        grads[part, high] = (grad_act * gate * sig).astype(BF)
        return carry

    lax.fori_loop(0, 4, hidden_grads, 0)
    for load in loads[3:8]:
        load.wait()
    outer = (((0,), (0,)), ((), ()))

    def in_grads(t, carry):
        rows = pl.ds(t * 256, 256)
        cols = pl.ds((t % 4) * 256, 256)
        grad = lax.dot_general(
            xv[t // 4, :, cols], grads[...], outer, preferred_element_type=F32
        ) * scale_in
        moment = momentum_beta * mgu[rows].astype(F32) + grad
        mgu[rows] = moment.astype(BF)
        lgu[rows] = (wgu[rows].astype(F32) - learn_rate * moment).astype(BF)
        for s in in_tile(t):
            s.start()
        return carry

    lax.fori_loop(0, 8, in_grads, 0)
    for load in loads[8:]:
        load.wait()

    def down_grads(c, carry):
        cols = pl.ds((c % 2) * 512, 512)
        where = pl.ds(c * 512, 512)
        grad = lax.dot_general(
            acv[...], yv[c // 2, :, cols], outer, preferred_element_type=F32
        ) * scale_hidden
        moment = momentum_beta * mdn[:, where].astype(F32) + grad
        mdn[:, where] = moment.astype(BF)
        ldn[:, where] = (wdn[:, where].astype(F32) - learn_rate * moment).astype(BF)
        for s in down_tile(c):
            s.start()
        return carry

    lax.fori_loop(0, 4, down_grads, 0)

    def back_rows(t, carry):
        part = pl.ds(t * 320, 320)
        inner = (((1,), (1,)), ((), ()))
        for r in range(2):
            back = lax.dot_general(
                grads[part], wgu[pl.ds(r * half, half)], inner, preferred_element_type=F32
            )
            xv[r, part] = (back * scale_in).astype(BF)
        return carry

    lax.fori_loop(0, 4, back_rows, 0)
    send_rows(1)
    moments = [
        pltpu.make_async_copy(s, d, go.at[i])
        for i, (s, d) in enumerate(((mgu, mgu_o), (mdn, md_o), (lgu, lgu_o), (ldn, ld_o)))
    ]
    for m in moments:
        m.start()

    def reduce(a):
        def body(i, carry):
            q = turn((i + 1) % 4)
            for r in range(2):
                group = (own[r] + q) % 4
                keep_copy(a, r, q).wait()
                for d in ORDER:
                    send_copy(a, r, q, d).wait_recv()
                hit, share = selection(mr, r, group)
                pick = (share if a == 0 else hit).astype(BF)
                for c in range(2):
                    part = pl.ds(c * (half // 2), half // 2)
                    rows = jnp.concatenate([rb[a, r, group, e, :, part] for e in range(4)], axis=0)
                    total = lax.dot_general(pick, rows, outer, preferred_element_type=F32)

                    @pl.when(i < 3)
                    def _():
                        qs[a, r, (q + 3) % 4, :, part] = total.astype(BF)

                    @pl.when(i == 3)
                    def _():
                        mine[r, :, part] = total

                @pl.when(i < 3)
                def _():
                    part_copy(a, r, q).start()
            return carry

        lax.fori_loop(0, 4, body, 0)
        there = pl.ds((1 - xh) * 128, 128)
        here = pl.ds(xh * 128, 128)
        for r in range(2):
            for q in ORDER:
                part_copy(a, r, q).wait_recv()
            away = mine[r, there]
            stay = mine[r, here]
            for q in ORDER:
                away = away + qr[a, r, q - 1, there].astype(F32)
                stay = stay + qr[a, r, q - 1, here].astype(F32)
            xsend[a, r] = away.astype(BF)
            x_copy(a, r).start()
            kept[a, r] = stay

    reduce(0)
    reduce(1)
    for a in range(2):
        for r in range(2):
            x_copy(a, r).wait_recv()
            total = kept[a, r] + xrecv[a, r].astype(F32)
            results[a][:, pl.ds(r * half, half)] = total.astype(BF)
    for a in range(2):
        for r in range(2):
            x_copy(a, r).wait_send()
            for q in range(4):
                for d in ORDER:
                    send_copy(a, r, q, d).wait_send()
            for q in ORDER:
                part_copy(a, r, q).wait_send()
    for t in range(8):
        for s in in_tile(t):
            s.wait()
    for c in range(4):
        for s in down_tile(c):
            s.wait()
    for m in moments:
        m.wait()


def combine(xi, yi, pr, gui, aci, mr, wg, wu, wd, mg, mu, md):
    half = xi.shape[2]
    width = 2 * half
    slots = xi.shape[1]
    hidden = wd.shape[0]
    dma = pltpu.SemaphoreType.DMA
    anywhere = pl.BlockSpec(memory_space=pl.ANY)
    vmem = pl.BlockSpec(memory_space=pltpu.VMEM)
    tokens = jax.ShapeDtypeStruct((128, width), BF)
    inward = jax.ShapeDtypeStruct((width, 2 * hidden), BF)
    down = jax.ShapeDtypeStruct((hidden, width), BF)
    return pl.pallas_call(
        combine_kernel,
        out_shape=(
            tokens, tokens, inward, down, inward, down,
            jax.ShapeDtypeStruct((2, width, 2 * hidden), BF),
            jax.ShapeDtypeStruct((2, hidden, width), BF),
        ),
        in_specs=[*[anywhere] * 5, vmem, *[anywhere] * 6],
        out_specs=(vmem, vmem, *[anywhere] * 6),
        scratch_shapes=[
            pltpu.VMEM((2, slots, half), BF),
            pltpu.VMEM((2, slots, half), BF),
            pltpu.VMEM((slots, 2 * hidden), F32),
            pltpu.VMEM((slots, hidden), BF),
            pltpu.VMEM((slots, 2 * hidden), BF),
            pltpu.VMEM((width, 2 * hidden), BF),
            pltpu.VMEM((hidden, width), BF),
            pltpu.VMEM((width, 2 * hidden), BF),
            pltpu.VMEM((hidden, width), BF),
            pltpu.VMEM((width, 2 * hidden), BF),
            pltpu.VMEM((hidden, width), BF),
            pltpu.VMEM((2, 2, 4, 4, 80, half), BF),
            pltpu.VMEM((2, 2, 3, 256, half), BF),
            pltpu.VMEM((2, 2, 3, 256, half), BF),
            pltpu.VMEM((2, 2, 128, half), BF),
            pltpu.VMEM((2, 2, 128, half), BF),
            pltpu.VMEM((2, 256, half), F32),
            pltpu.VMEM((2, 2, 128, half), F32),
            dma((2, 2, 4, 4)), dma((2, 2, 4, 4)),
            dma((2, 2, 4)),
            dma((2, 2, 4)), dma((2, 2, 4)),
            dma((2, 2)), dma((2, 2)),
            dma((2, 12)), dma((2, 12)),
            dma((10,)), dma((4,)),
        ],
        compiler_params=pltpu.CompilerParams(
            collective_id=1, has_side_effects=True, vmem_limit_bytes=63 * 2**20
        ),
        name="combine",
    )(xi, yi, pr, gui, aci, mr, wg, wu, wd, mg, mu, md)


def finish_kernel(
    bit, lgu, bgu, mgu, ld, bd, md, out, tg,
    ng, nu, nd, mgo, muo, mdo, oo, to,
):
    hidden = ng.shape[1]
    inward = ((lgu[...].astype(F32) + bgu[0].astype(F32)) * 0.5).astype(BF)
    ng[...] = inward[:, :hidden]
    nu[...] = inward[:, hidden:]
    nd[...] = ((ld[...].astype(F32) + bd[0].astype(F32)) * 0.5).astype(BF)
    mgo[...] = mgu[:, :hidden]
    muo[...] = mgu[:, hidden:]
    mdo[...] = md[...]
    oo[...] = out[...]
    to[...] = tg[...]


def finish(bit, lgu, bgu, mgu, ld, bd, md, out, tg):
    width, both = lgu.shape
    hidden = both // 2
    steps = 4
    tile = width // steps
    rows = pl.BlockSpec((tile, both), lambda i, b: (i, 0))
    half_rows = pl.BlockSpec((tile, hidden), lambda i, b: (i, 0))
    cols = pl.BlockSpec((hidden, tile), lambda i, b: (0, i))
    toks = pl.BlockSpec((128, tile), lambda i, b: (0, i))
    shape = jax.ShapeDtypeStruct
    return pl.pallas_call(
        finish_kernel,
        out_shape=(
            shape((width, hidden), BF), shape((width, hidden), BF), shape((hidden, width), BF),
            shape((width, hidden), BF), shape((width, hidden), BF), shape((hidden, width), BF),
            shape((128, width), BF), shape((128, width), BF),
        ),
        grid_spec=pltpu.PrefetchScalarGridSpec(
            num_scalar_prefetch=1,
            grid=(steps,),
            in_specs=[
                rows, pl.BlockSpec((1, tile, both), lambda i, b: (b[0], i, 0)), rows,
                cols, pl.BlockSpec((1, hidden, tile), lambda i, b: (b[0], 0, i)), cols,
                toks, toks,
            ],
            out_specs=(half_rows, half_rows, cols, half_rows, half_rows, cols, toks, toks),
        ),
        compiler_params=pltpu.CompilerParams(vmem_limit_bytes=62 * 2**20),
        name="finish",
    )(bit, lgu, bgu, mgu, ld, bd, md, out, tg)


def per_device(
    tokens, routing, gate_scores, cotangent,
    w_gate, w_up, w_down, mom_gate, mom_up, mom_down, gossip_round,
):
    wg, wu, wd = w_gate[0, 0], w_up[0, 0], w_down[0, 0]
    xi, yi, pr, gui, aci, meta = dispatch(
        tokens, cotangent, routing.T, gate_scores.T, wg, wu, wd
    )
    out, tg, lgu, ld, mgu, md, bgu, bd = combine(
        xi, yi, pr, gui, aci, meta, wg, wu, wd, mom_gate[0, 0], mom_up[0, 0], mom_down[0, 0]
    )
    ng, nu, nd, mg, mu, mdn, layer_out, token_grad = finish(
        gossip_round % 2, lgu, bgu, mgu, ld, bd, md, out, tg
    )
    return (
        layer_out, token_grad, ng[None, None], nu[None, None], nd[None, None],
        mg[None, None], mu[None, None], mdn[None, None],
    )


def solution(mesh):
    flat = P(("replica", "expert"), None)
    stacked = P("replica", "expert", None, None)
    return jax.shard_map(
        per_device,
        mesh=mesh,
        in_specs=(flat,) * 4 + (stacked,) * 6 + (P("expert"),),
        out_specs=(flat,) * 2 + (stacked,) * 6,
        check_vma=False,
    )
```

time: 314 us -> 267 us (0.85)
  matrix products: 45.7 us -> 0 us
  Pallas kernels: 247 us -> 262 us
  other arithmetic: 12.6 us -> 0 us
    dot_general x10 -> x0, matrix products: 45.7 us -> none  [the longest x1 8.35 us: expert_math(): lax.dot_general(rows_in, grad_up_pre, outer, preferred_element_type=F32)]
    pallas_call x2 -> x3, Pallas kernels: 247 us -> 262 us  [the longest x1 137 us: combine(): pl.pallas_call(combine_kernel, out_shape=(tokens, tokens, inward, down, i...]
    broadcast_in_dim x2 -> x0, other arithmetic: 9.15 us -> none  [per_device(): averaged.append(((local.astype(F32) + other) * 0.5).astype(BF)[None, None])]
where the time goes in v2:
time: 267 us; the launch traced here: 263 us
  Pallas kernels  262 us (98%)
    pallas_call x1, Pallas kernels, combine(): pl.pallas_call(combine_kernel, out_shape=(tokens, tokens, inward, down, i...  137 us
    pallas_call x1, Pallas kernels, dispatch(): pl.pallas_call(dispatch_kernel, out_shape=(halves, halves, halves, jax.Sh...  115 us
    pallas_call x1, Pallas kernels, finish(): pl.pallas_call(finish_kernel, out_shape=(shape((width, hidden), BF), shap...  9.41 us

profile of v2, /device:TPU:50, one launch (start us, length us, event | category | flops | bytes accessed | tf_op | source)
XLA Modules:
  0.0 263.0 jit_solution(5556678806440973225)
XLA Ops:
  1.3 115.4 %dispatch.1 = (bf16[2,1280,1024]{2,1,0:T(8,128)(2,1)}, bf16[2,1280,1024]{2,1,0:T(8,128)(2,1)}, bf16[2,1280,1024]{2,1,0:T(8,128)(2,1)}, f32[1280,768]{1,0:T(8,128...) custom-call(bf16[128,2048]{1,0:T(8,128)(2,1)} %tok.1, bf16[128,2048]{1,0:T(8,128)(2,1)} %cot.1, ...), custom_call_target="tpu_custom_call" | custom-call | tf_op jit(solution)/shard_map/dispatch/pallas_call | solution.py:305
  116.7 136.9 %combine.1 = (bf16[128,2048]{1,0:T(8,128)(2,1)}, bf16[128,2048]{1,0:T(8,128)(2,1)}, bf16[2048,768]{1,0:T(8,128)(2,1)}, bf16[384,2048]{1,0:T(8,128)(2,1)}, bf16[2...) custom-call(bf16[2,1280,1024]{2,1,0:T(8,128)(2,1)} %get-tuple-elemen, ...), custom_call_target="tpu_custom_call" | custom-call | tf_op jit(solution)/shard_map/combine/pallas_call | solution.py:581
  253.6 9.4 %finish.1 = (bf16[2048,384]{1,0:T(8,128)(2,1)}, bf16[2048,384]{1,0:T(8,128)(2,1)}, bf16[384,2048]{1,0:T(8,128)(2,1)}, bf16[2048,384]{1,0:T(8,128)(2,1)}, bf16[20...) custom-call(s32[1]{0:T(128)S(6)} %select_n.7.bit, ...), custom_call_target="tpu_custom_call" | custom-call | tf_op jit(solution)/shard_map/finish/pallas_call | solution.py:649

commit v3 on v2

--- a/solution.py
+++ b/solution.py
@@ -12,6 +12,7 @@
 BF = jnp.bfloat16
 F32 = jnp.float32
 ORDER = (1, 3, 2)
+NEAR = (1, 3)
 
 
 def place():
@@ -90,9 +91,9 @@
 
 def dispatch_kernel(
     tok, cot, rt, gt, wg, wu, wd,
-    xo, yo, po, guo, aco, mo,
-    ag, sb, xb, mr, m1, m2, wgu, wdn, gus, acs, prs,
-    ms, mrs, xs, xr, gs, gr, us, ur, ls, lo, os_, wl, fo,
+    xo, yo, po, aco, gro, mo,
+    ag, sb, xb, mr, m1, m2, wgu, wdn, gus, acs, prs, gas, grs,
+    ms, mrs, xs, xr, gs, gr, us, ur, ls, lo, os_, wl, fo, hs, hr, go, ks, kr,
 ):
     xh, z, y = place()
     half = ag.shape[-1]
@@ -123,6 +124,14 @@
         spot = ag.at[a, r, own[r], pl.ds(xh * 128, 128)]
         return remote(cols(a, r), spot, xs.at[a, r], xr.at[a, r], partner)
 
+    def cross_copy(r, q):
+        spot = ag.at[1, r, (own[r] + q) % 4, pl.ds(xh * 128, 128)]
+        return remote(spot, spot, ks.at[r, q], kr.at[r, q], partner)
+
+    def cross_wait(r, q):
+        spot = ag.at[1, r, (own[r] + q) % 4, pl.ds((1 - xh) * 128, 128)]
+        remote(spot, spot, ks.at[r, q], kr.at[r, q], partner).wait_recv()
+
     def own_copy(a, r):
         return pltpu.make_async_copy(
             cols(a, r), ag.at[a, r, own[r], pl.ds(xh * 128, 128)], ls.at[a, r]
@@ -143,6 +152,27 @@
         back = (4 - q) % 4
         remote(spot, spot, gs.at[a, r, h, back], gr.at[a, r, h, back], partner).wait_recv()
 
+    def relay_copy(a, r, h, side):
+        where = xh if h == 0 else 1 - xh
+        came, to = ((own[r] + 3) % 4, 1) if side == 0 else ((own[r] + 1) % 4, 3)
+        spot = ag.at[a, r, came, pl.ds(where * 128 + side * 64, 64)]
+        return remote(
+            spot, spot, hs.at[a, r, h, side], hr.at[a, r, h, side],
+            {"expert": peer(r, 0, xh, z, y, to)},
+        )
+
+    def relay_wait(a, r, h, side):
+        where = xh if h == 0 else 1 - xh
+        spot = ag.at[a, r, (own[r] + 2) % 4, pl.ds(where * 128 + side * 64, 64)]
+        remote(spot, spot, hs.at[a, r, h, side], hr.at[a, r, h, side], partner).wait_recv()
+
+    def relay(a, h):
+        for r in range(2):
+            gather_wait(a, r, h, 3)
+            relay_copy(a, r, h, 0).start()
+            gather_wait(a, r, h, 1)
+            relay_copy(a, r, h, 1).start()
+
     def landing(a, r, sender, group):
         row = (sender * 4 + group) if r == 0 else (group * 4 + sender)
         return xb.at[a, r, pl.ds(row * 80, 80)]
@@ -175,12 +205,15 @@
     for r in range(2):
         x_copy(0, r).start()
         own_copy(0, r).start()
-    for d in ORDER:
+    for d in NEAR:
         for r in range(2):
             gather_copy(0, r, 0, d).start()
     for r in range(2):
         x_copy(1, r).start()
         own_copy(1, r).start()
+    for d in NEAR:
+        for r in range(2):
+            gather_copy(1, r, 0, d).start()
     for load in loads:
         load.start()
     pairs = [(dx, d) for dx in range(2) for d in range(4) if dx or d]
@@ -196,13 +229,16 @@
             own_copy(a, r).wait()
             spot = ag.at[a, r, own[r], pl.ds((1 - xh) * 128, 128)]
             remote(spot, spot, xs.at[a, r], xr.at[a, r], partner).wait_recv()
-            for d in ORDER:
-                gather_copy(a, r, 1, d).start()
-
+            if a == 0:
+                for d in NEAR:
+                    gather_copy(a, r, 1, d).start()
+
+    relay(0, 0)
     pass_on(0)
-    for d in ORDER:
-        for r in range(2):
-            gather_copy(1, r, 0, d).start()
+    relay(1, 0)
+    for q in NEAR:
+        for r in range(2):
+            cross_copy(r, q).start()
     for r in range(2):
         for dx, d in pairs:
             meta_copy(r, dx, d).wait()
@@ -210,13 +246,36 @@
     def spread(a):
         def body(i, carry):
             q = turn(i)
+
+            if a == 0:
+
+                @pl.when(i == 1)
+                def _():
+                    relay(0, 1)
+
+                @pl.when(i == 2)
+                def _():
+                    for r in range(2):
+                        for side in range(2):
+                            relay_wait(1, r, 0, side)
+                        cross_copy(r, 2).start()
+
             for r in range(2):
                 group = (own[r] + q) % 4
 
-                @pl.when(i > 0)
-                def _():
-                    gather_wait(a, r, 0, q)
-                    gather_wait(a, r, 1, q)
+                if a == 0:
+
+                    @pl.when(i == 3)
+                    def _():
+                        for h in range(2):
+                            for side in range(2):
+                                relay_wait(0, r, h, side)
+
+                else:
+
+                    @pl.when(i > 0)
+                    def _():
+                        cross_wait(r, q)
 
                 hit, share = selection(mr, r, group)
                 hit = hit.astype(BF)
@@ -240,26 +299,28 @@
     spread(1)
     results = (xo, yo)
 
-    def arrive(a):
-        for r in range(2):
-            for q in range(4):
-                keep_copy(a, r, q).wait()
-                for d in ORDER:
-                    spread_copy(a, r, q, d).wait()
-            pltpu.make_async_copy(xb.at[a, r], results[a].at[r], os_.at[a, r]).start()
-
-    arrive(0)
+    def landed(a, r, q):
+        keep_copy(a, r, q).wait()
+        for d in ORDER:
+            spread_copy(a, r, q, d).wait()
+
+    def leave(a, r):
+        pltpu.make_async_copy(xb.at[a, r], results[a].at[r], os_.at[a, r]).start()
+
+    for r in range(2):
+        for q in range(4):
+            landed(0, r, q)
+        leave(0, r)
     for load in loads:
         load.wait()
 
     def stores(t):
         part = pl.ds(t * 320, 320)
         found = [
-            pltpu.make_async_copy(gus.at[part], guo.at[part], fo.at[t, 0]),
-            pltpu.make_async_copy(acs.at[part], aco.at[part], fo.at[t, 1]),
+            pltpu.make_async_copy(acs.at[part], aco.at[part], fo.at[t, 0]),
         ]
         for r in range(2):
-            found.append(pltpu.make_async_copy(prs.at[r, part], po.at[r, part], fo.at[t, 2 + r]))
+            found.append(pltpu.make_async_copy(prs.at[r, part], po.at[r, part], fo.at[t, 1 + r]))
         return found
 
     def forward(t, carry):
@@ -279,17 +340,63 @@
         return carry
 
     lax.fori_loop(0, 4, forward, 0)
-    arrive(1)
+    gas[...] = jnp.zeros_like(gas)
+    inner = (((1,), (1,)), ((), ()))
+
+    def grad_part(i, carry):
+        q = turn(i)
+        landed(1, 0, q)
+        spots = [pl.ds((k * 4 + (y + q) % 4) * 80, 80) for k in range(4)]
+        rows = jnp.concatenate([xb[1, 0, s] for s in spots], axis=0)
+        more = lax.dot_general(rows, wdn[:, pl.ds(0, half)], inner, preferred_element_type=F32)
+        for k, s in enumerate(spots):
+            gas[s] += more[k * 80 : k * 80 + 80]
+        landed(1, 1, q)
+        part = pl.ds(((z + q) % 4) * 320, 320)
+        gas[part] += lax.dot_general(
+            xb[1, 1, part], wdn[:, pl.ds(half, half)], inner, preferred_element_type=F32
+        )
+        return carry
+
+    lax.fori_loop(0, 4, grad_part, 0)
+    for r in range(2):
+        leave(1, r)
     mo[...] = mr[...]
+
+    def grad_store(t):
+        part = pl.ds(t * 160, 160)
+        return pltpu.make_async_copy(grs.at[part], gro.at[part], go.at[t])
+
+    def hidden_grads(t, carry):
+        part = pl.ds(t * 160, 160)
+        grad_act = gas[part] * scale_hidden
+        gate = gus[part, pl.ds(0, hidden)]
+        up = gus[part, pl.ds(hidden, hidden)]
+        sig = jax.nn.sigmoid(gate)
+        grs[part, pl.ds(0, hidden)] = (
+            grad_act * up * sig * (1.0 + gate * (1.0 - sig))
+        ).astype(BF)
+        grs[part, pl.ds(hidden, hidden)] = (grad_act * gate * sig).astype(BF)
+        grad_store(t).start()
+        return carry
+
+    lax.fori_loop(0, 8, hidden_grads, 0)
+    for t in range(8):
+        grad_store(t).wait()
+    for r in range(2):
+        for q in ORDER:
+            cross_copy(r, q).wait_send()
     for t in range(4):
         for s in stores(t):
             s.wait()
     for a in range(2):
         for r in range(2):
             x_copy(a, r).wait_send()
-            for h in range(2):
-                for d in ORDER:
+            for h in range(2 - a):
+                for d in NEAR:
                     gather_copy(a, r, h, d).wait_send()
+                for side in range(2):
+                    relay_copy(a, r, h, side).wait_send()
             pltpu.make_async_copy(xb.at[a, r], results[a].at[r], os_.at[a, r]).wait()
 
 
@@ -306,8 +413,8 @@
         dispatch_kernel,
         out_shape=(
             halves, halves, halves,
-            jax.ShapeDtypeStruct((slots, 2 * hidden), F32),
             jax.ShapeDtypeStruct((slots, hidden), BF),
+            jax.ShapeDtypeStruct((slots, 2 * hidden), BF),
             jax.ShapeDtypeStruct((2, 4, 2, 8, 128), F32),
         ),
         in_specs=[anywhere, anywhere, vmem, vmem, anywhere, anywhere, anywhere],
@@ -324,12 +431,16 @@
             pltpu.VMEM((slots, 2 * hidden), F32),
             pltpu.VMEM((slots, hidden), BF),
             pltpu.VMEM((2, slots, half), BF),
+            pltpu.VMEM((slots, hidden), F32),
+            pltpu.VMEM((slots, 2 * hidden), BF),
             dma((2, 2, 4)), dma((2, 2, 4)),
             dma((2, 2)), dma((2, 2)),
             dma((2, 2, 2, 4)), dma((2, 2, 2, 4)),
             dma((2, 2, 4, 4)), dma((2, 2, 4, 4)),
             dma((2, 2)), dma((2, 2, 4)), dma((2, 2)),
-            dma((3,)), dma((4, 4)),
+            dma((3,)), dma((4, 3)),
+            dma((2, 2, 2, 2)), dma((2, 2, 2, 2)), dma((8,)),
+            dma((2, 4)), dma((2, 4)),
         ],
         compiler_params=pltpu.CompilerParams(
             collective_id=0, has_side_effects=True, vmem_limit_bytes=60 * 2**20
@@ -339,9 +450,9 @@
 
 
 def combine_kernel(
-    xi, yi, pr, gui, aci, mr, wg, wu, wd, mg, mu, md,
+    xi, yi, pr, aci, gri, mr, wg, wu, wd, mg, mu, md,
     out, tg, lgu_o, ld_o, mgu_o, md_o, bgu, bd,
-    xv, yv, gup, acv, grads, wgu, wdn, mgu, mdn, lgu, ldn,
+    xv, yv, acv, grads, wgu, wdn, mgu, mdn, lgu, ldn,
     rb, qs, qr, xsend, xrecv, mine, kept,
     cs, cr, ls, ps, pt, xs, xr, ws, wr, wl, go,
 ):
@@ -352,10 +463,13 @@
     scale_in = (2 * half) ** (-0.5)
     scale_hidden = hidden ** (-0.5)
     low, high = pl.ds(0, hidden), pl.ds(hidden, hidden)
-    copies = [
-        (wd, wdn), (yi, yv), (gui, gup), (xi, xv), (wg, wgu.at[:, low]), (wu, wgu.at[:, high]),
-        (mg, mgu.at[:, low]), (mu, mgu.at[:, high]), (aci, acv), (md, mdn),
-    ]
+    copies = [(gri, grads)]
+    for k in range(2):
+        rows = pl.ds(k * half, half)
+        copies.append((xi.at[k], xv.at[k]))
+        for src, dst, cols in ((mg, mgu, low), (mu, mgu, high), (wg, wgu, low), (wu, wgu, high)):
+            copies.append((src.at[rows], dst.at[rows, cols]))
+    copies += [(aci, acv), (yi, yv), (md, mdn), (wd, wdn)]
     loads = [pltpu.make_async_copy(s, d, wl.at[i]) for i, (s, d) in enumerate(copies)]
     for load in loads:
         load.start()
@@ -423,32 +537,16 @@
         ]
 
     send_rows(0)
-    for load in loads[:3]:
-        load.wait()
-
-    def hidden_grads(t, carry):
-        part = pl.ds(t * 320, 320)
-        inner = (((1,), (1,)), ((), ()))
-        grad_act = lax.dot_general(
-            yv[0, part], wdn[:, pl.ds(0, half)], inner, preferred_element_type=F32
-        )
-        grad_act = grad_act + lax.dot_general(
-            yv[1, part], wdn[:, pl.ds(half, half)], inner, preferred_element_type=F32
-        )
-        grad_act = grad_act * scale_hidden
-        gate = gup[part, low]
-        up = gup[part, high]
-        sig = jax.nn.sigmoid(gate)
-        grads[part, low] = (grad_act * up * sig * (1.0 + gate * (1.0 - sig))).astype(BF)
-        grads[part, high] = (grad_act * gate * sig).astype(BF)
-        return carry
-
-    lax.fori_loop(0, 4, hidden_grads, 0)
-    for load in loads[3:8]:
+    for load in loads[:6]:
         load.wait()
     outer = (((0,), (0,)), ((), ()))
 
     def in_grads(t, carry):
+        @pl.when(t == 4)
+        def _():
+            for load in loads[6:11]:
+                load.wait()
+
         rows = pl.ds(t * 256, 256)
         cols = pl.ds((t % 4) * 256, 256)
         grad = lax.dot_general(
@@ -462,7 +560,7 @@
         return carry
 
     lax.fori_loop(0, 8, in_grads, 0)
-    for load in loads[8:]:
+    for load in loads[11:]:
         load.wait()
 
     def down_grads(c, carry):
@@ -567,7 +665,7 @@
         m.wait()
 
 
-def combine(xi, yi, pr, gui, aci, mr, wg, wu, wd, mg, mu, md):
+def combine(xi, yi, pr, aci, gri, mr, wg, wu, wd, mg, mu, md):
     half = xi.shape[2]
     width = 2 * half
     slots = xi.shape[1]
@@ -590,7 +688,6 @@
         scratch_shapes=[
             pltpu.VMEM((2, slots, half), BF),
             pltpu.VMEM((2, slots, half), BF),
-            pltpu.VMEM((slots, 2 * hidden), F32),
             pltpu.VMEM((slots, hidden), BF),
             pltpu.VMEM((slots, 2 * hidden), BF),
             pltpu.VMEM((width, 2 * hidden), BF),
@@ -611,13 +708,13 @@
             dma((2, 2, 4)), dma((2, 2, 4)),
             dma((2, 2)), dma((2, 2)),
             dma((2, 12)), dma((2, 12)),
-            dma((10,)), dma((4,)),
+            dma((15,)), dma((4,)),
         ],
         compiler_params=pltpu.CompilerParams(
             collective_id=1, has_side_effects=True, vmem_limit_bytes=63 * 2**20
         ),
         name="combine",
-    )(xi, yi, pr, gui, aci, mr, wg, wu, wd, mg, mu, md)
+    )(xi, yi, pr, aci, gri, mr, wg, wu, wd, mg, mu, md)
 
 
 def finish_kernel(
@@ -673,11 +770,11 @@
     w_gate, w_up, w_down, mom_gate, mom_up, mom_down, gossip_round,
 ):
     wg, wu, wd = w_gate[0, 0], w_up[0, 0], w_down[0, 0]
-    xi, yi, pr, gui, aci, meta = dispatch(
+    xi, yi, pr, aci, gri, meta = dispatch(
         tokens, cotangent, routing.T, gate_scores.T, wg, wu, wd
     )
     out, tg, lgu, ld, mgu, md, bgu, bd = combine(
-        xi, yi, pr, gui, aci, meta, wg, wu, wd, mom_gate[0, 0], mom_up[0, 0], mom_down[0, 0]
+        xi, yi, pr, aci, gri, meta, wg, wu, wd, mom_gate[0, 0], mom_up[0, 0], mom_down[0, 0]
     )
     ng, nu, nd, mg, mu, mdn, layer_out, token_grad = finish(
         gossip_round % 2, lgu, bgu, mgu, ld, bd, md, out, tg

time: 267 us -> 246 us (0.921)
  Pallas kernels: 262 us -> 241 us
    pallas_call x1, Pallas kernels: 115 us -> 99.7 us  [dispatch(): pl.pallas_call(dispatch_kernel, out_shape=(halves, halves, halves, jax.Sh...]
    pallas_call x1, Pallas kernels: 137 us -> 132 us  [combine(): pl.pallas_call(combine_kernel, out_shape=(tokens, tokens, inward, down, i...]
where the time goes in v3:
time: 246 us; the launch traced here: 243 us
  Pallas kernels  241 us (98%)
    pallas_call x1, Pallas kernels, combine(): pl.pallas_call(combine_kernel, out_shape=(tokens, tokens, inward, down, i...  132 us
    pallas_call x1, Pallas kernels, dispatch(): pl.pallas_call(dispatch_kernel, out_shape=(halves, halves, halves, jax.Sh...  99.7 us
    pallas_call x1, Pallas kernels, finish(): pl.pallas_call(finish_kernel, out_shape=(shape((width, hidden), BF), shap...  9.36 us

profile of v3, /device:TPU:50, one launch (start us, length us, event | category | flops | bytes accessed | tf_op | source)
XLA Modules:
  0.0 242.8 jit_solution(17416529931049841876)
XLA Ops:
  1.3 99.7 %dispatch.1 = (bf16[2,1280,1024]{2,1,0:T(8,128)(2,1)}, bf16[2,1280,1024]{2,1,0:T(8,128)(2,1)}, bf16[2,1280,1024]{2,1,0:T(8,128)(2,1)}, bf16[1280,384]{1,0:T(8,12...) custom-call(bf16[128,2048]{1,0:T(8,128)(2,1)} %tok.1, bf16[128,2048]{1,0:T(8,128)(2,1)} %cot.1, ...), custom_call_target="tpu_custom_call" | custom-call | tf_op jit(solution)/shard_map/dispatch/pallas_call | solution.py:412
  101.0 132.4 %combine.1 = (bf16[128,2048]{1,0:T(8,128)(2,1)}, bf16[128,2048]{1,0:T(8,128)(2,1)}, bf16[2048,768]{1,0:T(8,128)(2,1)}, bf16[384,2048]{1,0:T(8,128)(2,1)}, bf16[2...) custom-call(bf16[2,1280,1024]{2,1,0:T(8,128)(2,1)} %get-tuple-elemen, ...), custom_call_target="tpu_custom_call" | custom-call | tf_op jit(solution)/shard_map/combine/pallas_call | solution.py:679
  233.4 9.4 %finish.1 = (bf16[2048,384]{1,0:T(8,128)(2,1)}, bf16[2048,384]{1,0:T(8,128)(2,1)}, bf16[384,2048]{1,0:T(8,128)(2,1)}, bf16[2048,384]{1,0:T(8,128)(2,1)}, bf16[20...) custom-call(s32[1]{0:T(128)S(6)} %select_n.7.bit, ...), custom_call_target="tpu_custom_call" | custom-call | tf_op jit(solution)/shard_map/finish/pallas_call | solution.py:746

commit v4 on v3

--- a/solution.py
+++ b/solution.py
@@ -124,13 +124,13 @@
         spot = ag.at[a, r, own[r], pl.ds(xh * 128, 128)]
         return remote(cols(a, r), spot, xs.at[a, r], xr.at[a, r], partner)
 
-    def cross_copy(r, q):
-        spot = ag.at[1, r, (own[r] + q) % 4, pl.ds(xh * 128, 128)]
-        return remote(spot, spot, ks.at[r, q], kr.at[r, q], partner)
-
-    def cross_wait(r, q):
-        spot = ag.at[1, r, (own[r] + q) % 4, pl.ds((1 - xh) * 128, 128)]
-        remote(spot, spot, ks.at[r, q], kr.at[r, q], partner).wait_recv()
+    def cross_copy(a, r, q):
+        spot = ag.at[a, r, (own[r] + q) % 4, pl.ds(xh * 128, 128)]
+        return remote(spot, spot, ks.at[a, r, q], kr.at[a, r, q], partner)
+
+    def cross_wait(a, r, q):
+        spot = ag.at[a, r, (own[r] + q) % 4, pl.ds((1 - xh) * 128, 128)]
+        remote(spot, spot, ks.at[a, r, q], kr.at[a, r, q], partner).wait_recv()
 
     def own_copy(a, r):
         return pltpu.make_async_copy(
@@ -152,26 +152,24 @@
         back = (4 - q) % 4
         remote(spot, spot, gs.at[a, r, h, back], gr.at[a, r, h, back], partner).wait_recv()
 
-    def relay_copy(a, r, h, side):
-        where = xh if h == 0 else 1 - xh
+    def relay_copy(a, r, side):
         came, to = ((own[r] + 3) % 4, 1) if side == 0 else ((own[r] + 1) % 4, 3)
-        spot = ag.at[a, r, came, pl.ds(where * 128 + side * 64, 64)]
+        spot = ag.at[a, r, came, pl.ds(xh * 128 + side * 64, 64)]
         return remote(
-            spot, spot, hs.at[a, r, h, side], hr.at[a, r, h, side],
+            spot, spot, hs.at[a, r, side], hr.at[a, r, side],
             {"expert": peer(r, 0, xh, z, y, to)},
         )
 
-    def relay_wait(a, r, h, side):
-        where = xh if h == 0 else 1 - xh
-        spot = ag.at[a, r, (own[r] + 2) % 4, pl.ds(where * 128 + side * 64, 64)]
-        remote(spot, spot, hs.at[a, r, h, side], hr.at[a, r, h, side], partner).wait_recv()
-
-    def relay(a, h):
-        for r in range(2):
-            gather_wait(a, r, h, 3)
-            relay_copy(a, r, h, 0).start()
-            gather_wait(a, r, h, 1)
-            relay_copy(a, r, h, 1).start()
+    def relay_wait(a, r, side):
+        spot = ag.at[a, r, (own[r] + 2) % 4, pl.ds(xh * 128 + side * 64, 64)]
+        remote(spot, spot, hs.at[a, r, side], hr.at[a, r, side], partner).wait_recv()
+
+    def relay(a):
+        for r in range(2):
+            gather_wait(a, r, 0, 3)
+            relay_copy(a, r, 0).start()
+            gather_wait(a, r, 0, 1)
+            relay_copy(a, r, 1).start()
 
     def landing(a, r, sender, group):
         row = (sender * 4 + group) if r == 0 else (group * 4 + sender)
@@ -233,12 +231,19 @@
                 for d in NEAR:
                     gather_copy(a, r, 1, d).start()
 
-    relay(0, 0)
+    def cross_far(a):
+        for r in range(2):
+            for side in range(2):
+                relay_wait(a, r, side)
+            cross_copy(a, r, 2).start()
+
+    relay(0)
     pass_on(0)
-    relay(1, 0)
+    cross_far(0)
+    relay(1)
     for q in NEAR:
         for r in range(2):
-            cross_copy(r, q).start()
+            cross_copy(1, r, q).start()
     for r in range(2):
         for dx, d in pairs:
             meta_copy(r, dx, d).wait()
@@ -251,14 +256,13 @@
 
                 @pl.when(i == 1)
                 def _():
-                    relay(0, 1)
+                    for r in range(2):
+                        for k in NEAR:
+                            gather_wait(0, r, 1, k)
 
                 @pl.when(i == 2)
                 def _():
-                    for r in range(2):
-                        for side in range(2):
-                            relay_wait(1, r, 0, side)
-                        cross_copy(r, 2).start()
+                    cross_far(1)
 
             for r in range(2):
                 group = (own[r] + q) % 4
@@ -267,15 +271,13 @@
 
                     @pl.when(i == 3)
                     def _():
-                        for h in range(2):
-                            for side in range(2):
-                                relay_wait(0, r, h, side)
+                        cross_wait(0, r, 2)
 
                 else:
 
                     @pl.when(i > 0)
                     def _():
-                        cross_wait(r, q)
+                        cross_wait(1, r, q)
 
                 hit, share = selection(mr, r, group)
                 hit = hit.astype(BF)
@@ -384,8 +386,9 @@
     for t in range(8):
         grad_store(t).wait()
     for r in range(2):
+        cross_copy(0, r, 2).wait_send()
         for q in ORDER:
-            cross_copy(r, q).wait_send()
+            cross_copy(1, r, q).wait_send()
     for t in range(4):
         for s in stores(t):
             s.wait()
@@ -395,8 +398,8 @@
             for h in range(2 - a):
                 for d in NEAR:
                     gather_copy(a, r, h, d).wait_send()
-                for side in range(2):
-                    relay_copy(a, r, h, side).wait_send()
+            for side in range(2):
+                relay_copy(a, r, side).wait_send()
             pltpu.make_async_copy(xb.at[a, r], results[a].at[r], os_.at[a, r]).wait()
 
 
@@ -439,8 +442,8 @@
             dma((2, 2, 4, 4)), dma((2, 2, 4, 4)),
             dma((2, 2)), dma((2, 2, 4)), dma((2, 2)),
             dma((3,)), dma((4, 3)),
-            dma((2, 2, 2, 2)), dma((2, 2, 2, 2)), dma((8,)),
-            dma((2, 4)), dma((2, 4)),
+            dma((2, 2, 2)), dma((2, 2, 2)), dma((8,)),
+            dma((2, 2, 4)), dma((2, 2, 4)),
         ],
         compiler_params=pltpu.CompilerParams(
             collective_id=0, has_side_effects=True, vmem_limit_bytes=60 * 2**20
@@ -450,11 +453,11 @@
 
 
 def combine_kernel(
-    xi, yi, pr, aci, gri, mr, wg, wu, wd, mg, mu, md,
-    out, tg, lgu_o, ld_o, mgu_o, md_o, bgu, bd,
-    xv, yv, acv, grads, wgu, wdn, mgu, mdn, lgu, ldn,
+    bit, xi, yi, pr, aci, gri, mr, wg, wu, wd, mg, mu, md,
+    out, tg, ngu_o, nd_o, mgu_o, md_o, bgu, bd,
+    xv, yv, acv, grads, wgu, wdn, mgu, mdn, lgu, ldn, fgu, fdn,
     rb, qs, qr, xsend, xrecv, mine, kept,
-    cs, cr, ls, ps, pt, xs, xr, ws, wr, wl, go,
+    cs, cr, ls, ps, pt, xs, xr, ws, wr, wl, go, nl, av,
 ):
     xh, z, y = place()
     rep = lax.axis_index("replica")
@@ -524,16 +527,16 @@
         rows = pl.ds(t * 256, 256)
         src = lgu.at[rows]
         return [
-            remote(src, bgu.at[1, rows], ws.at[1, t], wr.at[1, t], far_mate),
-            remote(src, bgu.at[0, rows], ws.at[0, t], wr.at[0, t], core_mate),
+            remote(src, fgu.at[rows], ws.at[1, t], wr.at[1, t], far_mate),
+            remote(src, bgu.at[rows], ws.at[0, t], wr.at[0, t], core_mate),
         ]
 
     def down_tile(c):
         cols = pl.ds(c * 512, 512)
         src = ldn.at[:, cols]
         return [
-            remote(src, bd.at[1, :, cols], ws.at[1, 8 + c], wr.at[1, 8 + c], far_mate),
-            remote(src, bd.at[0, :, cols], ws.at[0, 8 + c], wr.at[0, 8 + c], core_mate),
+            remote(src, fdn.at[:, cols], ws.at[1, 8 + c], wr.at[1, 8 + c], far_mate),
+            remote(src, bd.at[:, cols], ws.at[0, 8 + c], wr.at[0, 8 + c], core_mate),
         ]
 
     send_rows(0)
@@ -592,7 +595,7 @@
     send_rows(1)
     moments = [
         pltpu.make_async_copy(s, d, go.at[i])
-        for i, (s, d) in enumerate(((mgu, mgu_o), (mdn, md_o), (lgu, lgu_o), (ldn, ld_o)))
+        for i, (s, d) in enumerate(((mgu, mgu_o), (mdn, md_o)))
     ]
     for m in moments:
         m.start()
@@ -641,7 +644,51 @@
             kept[a, r] = stay
 
     reduce(0)
+    for t in range(8):
+        in_tile(t)[1].wait_recv()
+    for c in range(4):
+        down_tile(c)[1].wait_recv()
+    near = [
+        pltpu.make_async_copy(bgu, wgu, nl.at[0]),
+        pltpu.make_async_copy(bd, wdn, nl.at[1]),
+    ]
+    for n in near:
+        n.start()
     reduce(1)
+    for n in near:
+        n.wait()
+    pick = bit[0] % 2 == 0
+
+    def in_store(t):
+        rows = pl.ds(t * 256, 256)
+        return pltpu.make_async_copy(lgu.at[rows], ngu_o.at[rows], av.at[t])
+
+    def down_store(c):
+        cols = pl.ds(c * 512, 512)
+        return pltpu.make_async_copy(ldn.at[:, cols], nd_o.at[:, cols], av.at[8 + c])
+
+    def in_average(t, carry):
+        far, close = in_tile(t)
+        far.wait()
+        close.wait_send()
+        rows = pl.ds(t * 256, 256)
+        other = jnp.where(pick, wgu[rows].astype(F32), fgu[rows].astype(F32))
+        lgu[rows] = ((lgu[rows].astype(F32) + other) * 0.5).astype(BF)
+        in_store(t).start()
+        return carry
+
+    def down_average(c, carry):
+        far, close = down_tile(c)
+        far.wait()
+        close.wait_send()
+        cols = pl.ds(c * 512, 512)
+        other = jnp.where(pick, wdn[:, cols].astype(F32), fdn[:, cols].astype(F32))
+        ldn[:, cols] = ((ldn[:, cols].astype(F32) + other) * 0.5).astype(BF)
+        down_store(c).start()
+        return carry
+
+    lax.fori_loop(0, 8, in_average, 0)
+    lax.fori_loop(0, 4, down_average, 0)
     for a in range(2):
         for r in range(2):
             x_copy(a, r).wait_recv()
@@ -656,16 +703,14 @@
             for q in ORDER:
                 part_copy(a, r, q).wait_send()
     for t in range(8):
-        for s in in_tile(t):
-            s.wait()
+        in_store(t).wait()
     for c in range(4):
-        for s in down_tile(c):
-            s.wait()
+        down_store(c).wait()
     for m in moments:
         m.wait()
 
 
-def combine(xi, yi, pr, aci, gri, mr, wg, wu, wd, mg, mu, md):
+def combine(bit, xi, yi, pr, aci, gri, mr, wg, wu, wd, mg, mu, md):
     half = xi.shape[2]
     width = 2 * half
     slots = xi.shape[1]
@@ -679,17 +724,17 @@
     return pl.pallas_call(
         combine_kernel,
         out_shape=(
-            tokens, tokens, inward, down, inward, down,
-            jax.ShapeDtypeStruct((2, width, 2 * hidden), BF),
-            jax.ShapeDtypeStruct((2, hidden, width), BF),
+            tokens, tokens, inward, down, inward, down, inward, down,
         ),
-        in_specs=[*[anywhere] * 5, vmem, *[anywhere] * 6],
+        in_specs=[pl.BlockSpec(memory_space=pltpu.SMEM), *[anywhere] * 5, vmem, *[anywhere] * 6],
         out_specs=(vmem, vmem, *[anywhere] * 6),
         scratch_shapes=[
             pltpu.VMEM((2, slots, half), BF),
             pltpu.VMEM((2, slots, half), BF),
             pltpu.VMEM((slots, hidden), BF),
             pltpu.VMEM((slots, 2 * hidden), BF),
+            pltpu.VMEM((width, 2 * hidden), BF),
+            pltpu.VMEM((hidden, width), BF),
             pltpu.VMEM((width, 2 * hidden), BF),
             pltpu.VMEM((hidden, width), BF),
             pltpu.VMEM((width, 2 * hidden), BF),
@@ -708,41 +753,56 @@
             dma((2, 2, 4)), dma((2, 2, 4)),
             dma((2, 2)), dma((2, 2)),
             dma((2, 12)), dma((2, 12)),
-            dma((15,)), dma((4,)),
+            dma((15,)), dma((2,)), dma((2,)), dma((12,)),
         ],
         compiler_params=pltpu.CompilerParams(
             collective_id=1, has_side_effects=True, vmem_limit_bytes=63 * 2**20
         ),
         name="combine",
-    )(xi, yi, pr, aci, gri, mr, wg, wu, wd, mg, mu, md)
+    )(bit, xi, yi, pr, aci, gri, mr, wg, wu, wd, mg, mu, md)
 
 
 def finish_kernel(
-    bit, lgu, bgu, mgu, ld, bd, md, out, tg,
-    ng, nu, nd, mgo, muo, mdo, oo, to,
+    ngu, mgu, nd, md, out, tg, ngo, nuo, ndo, mgo, muo, mdo, oo, to,
+    v0, v1, v2, v3, v4, v5, gets, puts,
 ):
-    hidden = ng.shape[1]
-    inward = ((lgu[...].astype(F32) + bgu[0].astype(F32)) * 0.5).astype(BF)
-    ng[...] = inward[:, :hidden]
-    nu[...] = inward[:, hidden:]
-    nd[...] = ((ld[...].astype(F32) + bd[0].astype(F32)) * 0.5).astype(BF)
-    mgo[...] = mgu[:, :hidden]
-    muo[...] = mgu[:, hidden:]
-    mdo[...] = md[...]
-    oo[...] = out[...]
-    to[...] = tg[...]
-
-
-def finish(bit, lgu, bgu, mgu, ld, bd, md, out, tg):
-    width, both = lgu.shape
+    hidden = ngo.shape[1]
+    whole = pl.ds(0, nd.shape[1])
+    left, right = pl.ds(0, hidden), pl.ds(hidden, hidden)
+    parts = 4
+    pieces = []
+    for k in range(parts):
+        for src, buf, ends in (
+            (ngu, v0, ((left, ngo), (right, nuo))), (mgu, v1, ((left, mgo), (right, muo))),
+            (nd, v2, ((whole, ndo),)), (md, v3, ((whole, mdo),)),
+            (out, v4, ((whole, oo),)), (tg, v5, ((whole, to),)),
+        ):
+            size = src.shape[0] // parts
+            pieces.append((src, buf, pl.ds(k * size, size), ends))
+    loads, stores = [], []
+    for n, (src, buf, rows, ends) in enumerate(pieces):
+        loads.append(pltpu.make_async_copy(src.at[rows], buf.at[rows], gets.at[n]))
+        stores.append([
+            pltpu.make_async_copy(buf.at[rows, cols], dst.at[rows], puts.at[n, i])
+            for i, (cols, dst) in enumerate(ends)
+        ])
+    for load in loads:
+        load.start()
+    for load, ends in zip(loads, stores):
+        load.wait()
+        for store in ends:
+            store.start()
+    for ends in stores:
+        for store in ends:
+            store.wait()
+
+
+def finish(ngu, mgu, nd, md, out, tg):
+    width, both = ngu.shape
     hidden = both // 2
-    steps = 4
-    tile = width // steps
-    rows = pl.BlockSpec((tile, both), lambda i, b: (i, 0))
-    half_rows = pl.BlockSpec((tile, hidden), lambda i, b: (i, 0))
-    cols = pl.BlockSpec((hidden, tile), lambda i, b: (0, i))
-    toks = pl.BlockSpec((128, tile), lambda i, b: (0, i))
     shape = jax.ShapeDtypeStruct
+    anywhere = pl.BlockSpec(memory_space=pl.ANY)
+    inputs = (ngu, mgu, nd, md, out, tg)
     return pl.pallas_call(
         finish_kernel,
         out_shape=(
@@ -750,19 +810,15 @@
             shape((width, hidden), BF), shape((width, hidden), BF), shape((hidden, width), BF),
             shape((128, width), BF), shape((128, width), BF),
         ),
-        grid_spec=pltpu.PrefetchScalarGridSpec(
-            num_scalar_prefetch=1,
-            grid=(steps,),
-            in_specs=[
-                rows, pl.BlockSpec((1, tile, both), lambda i, b: (b[0], i, 0)), rows,
-                cols, pl.BlockSpec((1, hidden, tile), lambda i, b: (b[0], 0, i)), cols,
-                toks, toks,
-            ],
-            out_specs=(half_rows, half_rows, cols, half_rows, half_rows, cols, toks, toks),
-        ),
+        in_specs=[anywhere] * 6,
+        out_specs=(anywhere,) * 8,
+        scratch_shapes=[
+            *[pltpu.VMEM(v.shape, BF) for v in inputs],
+            pltpu.SemaphoreType.DMA((24,)), pltpu.SemaphoreType.DMA((24, 2)),
+        ],
         compiler_params=pltpu.CompilerParams(vmem_limit_bytes=62 * 2**20),
         name="finish",
-    )(bit, lgu, bgu, mgu, ld, bd, md, out, tg)
+    )(*inputs)
 
 
 def per_device(
@@ -773,12 +829,11 @@
     xi, yi, pr, aci, gri, meta = dispatch(
         tokens, cotangent, routing.T, gate_scores.T, wg, wu, wd
     )
-    out, tg, lgu, ld, mgu, md, bgu, bd = combine(
-        xi, yi, pr, aci, gri, meta, wg, wu, wd, mom_gate[0, 0], mom_up[0, 0], mom_down[0, 0]
+    out, tg, ngu, nd, mgu, md, _, _ = combine(
+        gossip_round, xi, yi, pr, aci, gri, meta, wg, wu, wd,
+        mom_gate[0, 0], mom_up[0, 0], mom_down[0, 0],
     )
-    ng, nu, nd, mg, mu, mdn, layer_out, token_grad = finish(
-        gossip_round % 2, lgu, bgu, mgu, ld, bd, md, out, tg
-    )
+    ng, nu, nd, mg, mu, mdn, layer_out, token_grad = finish(ngu, mgu, nd, md, out, tg)
     return (
         layer_out, token_grad, ng[None, None], nu[None, None], nd[None, None],
         mg[None, None], mu[None, None], mdn[None, None],

time: 246 us -> 243 us (0.988)
    pallas_call x1, Pallas kernels: 99.7 us -> 97.2 us  [dispatch(): pl.pallas_call(dispatch_kernel, out_shape=(halves, halves, halves, jax.Sh...]
where the time goes in v4:
time: 243 us; the launch traced here: 241 us
  Pallas kernels  240 us (99%)
    pallas_call x1, Pallas kernels, combine(): pl.pallas_call(combine_kernel, out_shape=(tokens, tokens, inward, down, i...  134 us
    pallas_call x1, Pallas kernels, dispatch(): pl.pallas_call(dispatch_kernel, out_shape=(halves, halves, halves, jax.Sh...  97.2 us
    pallas_call x1, Pallas kernels, finish(): pl.pallas_call(finish_kernel, out_shape=(shape((width, hidden), BF), shap...  8.34 us

profile of v4, /device:TPU:50, one launch (start us, length us, event | category | flops | bytes accessed | tf_op | source)
XLA Modules:
  0.0 240.9 jit_solution(3396041042311817723)
XLA Ops:
  1.3 97.2 %dispatch.1 = (bf16[2,1280,1024]{2,1,0:T(8,128)(2,1)}, bf16[2,1280,1024]{2,1,0:T(8,128)(2,1)}, bf16[2,1280,1024]{2,1,0:T(8,128)(2,1)}, bf16[1280,384]{1,0:T(8,12...) custom-call(bf16[128,2048]{1,0:T(8,128)(2,1)} %tok.1, bf16[128,2048]{1,0:T(8,128)(2,1)} %cot.1, ...), custom_call_target="tpu_custom_call" | custom-call | tf_op jit(solution)/shard_map/dispatch/pallas_call | solution.py:415
  98.5 134.0 %combine.1 = (bf16[128,2048]{1,0:T(8,128)(2,1)}, bf16[128,2048]{1,0:T(8,128)(2,1)}, bf16[2048,768]{1,0:T(8,128)(2,1)}, bf16[384,2048]{1,0:T(8,128)(2,1)}, bf16[2...) custom-call(s32[1]{0:T(128)S(6)} %copy.19.bit, ...), custom_call_target="tpu_custom_call" | custom-call | tf_op jit(solution)/shard_map/combine/pallas_call | solution.py:724
  232.5 8.3 %finish.1 = (bf16[2048,384]{1,0:T(8,128)(2,1)}, bf16[2048,384]{1,0:T(8,128)(2,1)}, bf16[384,2048]{1,0:T(8,128)(2,1)}, bf16[2048,384]{1,0:T(8,128)(2,1)}, bf16[20...) custom-call(bf16[2048,768]{1,0:T(8,128)(2,1)} %get-tuple-element.34.ngu, ...), custom_call_target="tpu_custom_call" | custom-call | tf_op jit(solution)/shard_map/finish/pallas_call | solution.py:806

commit v5 on v4

--- a/solution.py
+++ b/solution.py
@@ -93,7 +93,7 @@
     tok, cot, rt, gt, wg, wu, wd,
     xo, yo, po, aco, gro, mo,
     ag, sb, xb, mr, m1, m2, wgu, wdn, gus, acs, prs, gas, grs,
-    ms, mrs, xs, xr, gs, gr, us, ur, ls, lo, os_, wl, fo, hs, hr, go, ks, kr,
+    ms, mrs, xs, xr, gs, gr, us, ur, ls, lo, os_, wl, fo, hs, hr, go, ks, kr, lv,
 ):
     xh, z, y = place()
     half = ag.shape[-1]
@@ -345,15 +345,25 @@
     gas[...] = jnp.zeros_like(gas)
     inner = (((1,), (1,)), ((), ()))
 
+    def leave_part(q, k):
+        if k < 4:
+            spot, r = pl.ds((k * 4 + (y + q) % 4) * 80, 80), 0
+        else:
+            spot, r = pl.ds(((z + q) % 4) * 320, 320), 1
+        return pltpu.make_async_copy(xb.at[1, r, spot], yo.at[r, spot], lv.at[q, k])
+
     def grad_part(i, carry):
         q = turn(i)
         landed(1, 0, q)
+        for k in range(4):
+            leave_part(q, k).start()
         spots = [pl.ds((k * 4 + (y + q) % 4) * 80, 80) for k in range(4)]
         rows = jnp.concatenate([xb[1, 0, s] for s in spots], axis=0)
         more = lax.dot_general(rows, wdn[:, pl.ds(0, half)], inner, preferred_element_type=F32)
         for k, s in enumerate(spots):
             gas[s] += more[k * 80 : k * 80 + 80]
         landed(1, 1, q)
+        leave_part(q, 4).start()
         part = pl.ds(((z + q) % 4) * 320, 320)
         gas[part] += lax.dot_general(
             xb[1, 1, part], wdn[:, pl.ds(half, half)], inner, preferred_element_type=F32
@@ -361,8 +371,6 @@
         return carry
 
     lax.fori_loop(0, 4, grad_part, 0)
-    for r in range(2):
-        leave(1, r)
     mo[...] = mr[...]
 
     def grad_store(t):
@@ -400,7 +408,11 @@
                     gather_copy(a, r, h, d).wait_send()
             for side in range(2):
                 relay_copy(a, r, side).wait_send()
-            pltpu.make_async_copy(xb.at[a, r], results[a].at[r], os_.at[a, r]).wait()
+            if a == 0:
+                pltpu.make_async_copy(xb.at[a, r], results[a].at[r], os_.at[a, r]).wait()
+    for q in range(4):
+        for k in range(5):
+            leave_part(q, k).wait()
 
 
 def dispatch(tokens, cotangent, rt, gt, wg, wu, wd):
@@ -443,7 +455,7 @@
             dma((2, 2)), dma((2, 2, 4)), dma((2, 2)),
             dma((3,)), dma((4, 3)),
             dma((2, 2, 2)), dma((2, 2, 2)), dma((8,)),
-            dma((2, 2, 4)), dma((2, 2, 4)),
+            dma((2, 2, 4)), dma((2, 2, 4)), dma((4, 5)),
         ],
         compiler_params=pltpu.CompilerParams(
             collective_id=0, has_side_effects=True, vmem_limit_bytes=60 * 2**20

time: 243 us -> 242 us (level)
  no operation moved by 1% of the time
where the time goes in v5:
time: 242 us; the launch traced here: 240 us
  Pallas kernels  239 us (99%)
    pallas_call x1, Pallas kernels, combine(): pl.pallas_call(combine_kernel, out_shape=(tokens, tokens, inward, down, i...  134 us
    pallas_call x1, Pallas kernels, dispatch(): pl.pallas_call(dispatch_kernel, out_shape=(halves, halves, halves, jax.Sh...  96.6 us
    pallas_call x1, Pallas kernels, finish(): pl.pallas_call(finish_kernel, out_shape=(shape((width, hidden), BF), shap...  8.34 us

profile of v5, /device:TPU:50, one launch (start us, length us, event | category | flops | bytes accessed | tf_op | source)
XLA Modules:
  0.0 240.2 jit_solution(5054656365201705373)
XLA Ops:
  1.3 96.6 %dispatch.1 = (bf16[2,1280,1024]{2,1,0:T(8,128)(2,1)}, bf16[2,1280,1024]{2,1,0:T(8,128)(2,1)}, bf16[2,1280,1024]{2,1,0:T(8,128)(2,1)}, bf16[1280,384]{1,0:T(8,12...) custom-call(bf16[128,2048]{1,0:T(8,128)(2,1)} %tok.1, bf16[128,2048]{1,0:T(8,128)(2,1)} %cot.1, ...), custom_call_target="tpu_custom_call" | custom-call | tf_op jit(solution)/shard_map/dispatch/pallas_call | solution.py:427
  97.9 134.0 %combine.1 = (bf16[128,2048]{1,0:T(8,128)(2,1)}, bf16[128,2048]{1,0:T(8,128)(2,1)}, bf16[2048,768]{1,0:T(8,128)(2,1)}, bf16[384,2048]{1,0:T(8,128)(2,1)}, bf16[2...) custom-call(s32[1]{0:T(128)S(6)} %copy.19.bit, ...), custom_call_target="tpu_custom_call" | custom-call | tf_op jit(solution)/shard_map/combine/pallas_call | solution.py:736
  231.8 8.3 %finish.1 = (bf16[2048,384]{1,0:T(8,128)(2,1)}, bf16[2048,384]{1,0:T(8,128)(2,1)}, bf16[384,2048]{1,0:T(8,128)(2,1)}, bf16[2048,384]{1,0:T(8,128)(2,1)}, bf16[20...) custom-call(bf16[2048,768]{1,0:T(8,128)(2,1)} %get-tuple-element.34.ngu, ...), custom_call_target="tpu_custom_call" | custom-call | tf_op jit(solution)/shard_map/finish/pallas_call | solution.py:818
